TPU v7x, 768 devices: a whole 4x8x12 slice. The times are simulated.
768 devices in a mesh: lat: 48 (over x, z), lev: 16 (over y, core).
Axes of the slice: x: 4, y: 8, z: 12, core: 2. Of those that a mesh axis runs over, the one named last changes fastest.
Arguments:
- grid_field: bfloat16 [32, 30720, 128], P('lev', 'lat'), may hold values from -6 to 6
- send_blocks: int32 [48, 2, 128], P('lat'), may hold values from 0 to 639
- donor_index: int32 [30720, 2], P('lat'), may hold values from 0 to 895
- tile_choice: int32 [30720, 2], P('lat'), may hold values from 0 to 7
- kernel_tiles: bfloat16 [8, 128, 128], replicated, may hold values from -0.375 to 0.375
- circle_len: int32 [768], replicated, may hold values from 20 to 5120, as said below
- slot_wave: int32 [1536], replicated, may hold values from 0 to 1535, each once
- legendre: bfloat16 [1536, 768, 1280], P(('lat', 'lev')), may hold values from -0.0024414062 to 0.0024414062
Outputs:
- spectra: bfloat16 [32, 2, 1536, 1280], P(None, None, ('lat', 'lev'))
Inputs may be any that keep to these rules, and one draw needn't show every extreme that they name: `circle_len`: each circle has 4 i + 16 points for a whole i of 1 or more, and some circle has 5120.
All inputs are finite; a program needn't handle non-finite values.
Results may differ from a plain program's by a relative error of at most 0.007.
Values may be sent and summed in bfloat16 or wider, within the bound.
A program may use at most 64 MiB of HBM per device.

v0:
```python
import math

import jax
import jax.numpy as jnp
from jax import lax
from jax.sharding import PartitionSpec as P

PTS = 5120


def extended(array, sides, width):
    for axis, dim in sides:
        size, length = (lax.axis_size(axis), array.shape[dim])
        up = [(i, (i + 1) % size) for i in range(size - 1)]
        down = [(j, i) for i, j in up]
        last = lax.slice_in_dim(array, length - width, length, axis=dim)
        leading = lax.slice_in_dim(array, 0, width, axis=dim)
        before = lax.ppermute(last, axis, up)
        after = lax.ppermute(leading, axis, down)
        array = jnp.concatenate([before, array, after], axis=dim)
    return array


def circle_table(length, waves, points, top_wave):
    live_slot = (waves >= 1) & (waves < top_wave) & (2 * waves < length)
    step_angle = 2.0 * math.pi / length.astype(jnp.float32)
    coarse = jnp.arange(points // 128, dtype=jnp.int32) * 128
    fine_pos = jnp.arange(128, dtype=jnp.int32)
    angle_hi = (coarse[:, None] * waves[None, :] % length).astype(jnp.float32) * step_angle
    lower_angle = (fine_pos[:, None] * waves[None, :] % length).astype(jnp.float32) * step_angle
    cos_hi = jnp.cos(angle_hi)[:, None, :]
    sin_hi = jnp.sin(angle_hi)[:, None, :]
    cos_lo = jnp.cos(lower_angle)[None]
    sin_lo = jnp.sin(lower_angle)[None]
    cosine = (cos_hi * cos_lo - sin_hi * sin_lo).reshape(points, -1)
    sine_part = (sin_hi * cos_lo + cos_hi * sin_lo).reshape(points, -1)
    keep_mask = (jnp.arange(points, dtype=jnp.int32) < length)[:, None] & live_slot[None, :]
    return jnp.concatenate(
        [jnp.where(keep_mask, cosine, 0.0), jnp.where(keep_mask, -sine_part, 0.0)], axis=1
    ).astype(jnp.bfloat16)


def transform(values, lengths, waves, top_wave):
    row_count = values.shape[0]
    points = values.shape[2]
    slot_count = waves.shape[0]
    blocks = slot_count // 128
    wave_blocks = waves.reshape(blocks, 128)

    def per_circle(operands):
        circle_vals, length = operands

        def per_block(wave_part):
            factors = circle_table(length, wave_part, points, top_wave)
            return jnp.dot(circle_vals, factors, preferred_element_type=jnp.float32).astype(
                jnp.bfloat16
            )

        pieces = lax.map(per_block, wave_blocks)
        return (
            pieces.reshape(blocks, row_count, 2, 128)
            .transpose(1, 2, 0, 3)
            .reshape(row_count, 2, slot_count)
        )

    result = lax.map(per_circle, (jnp.moveaxis(values, 1, 0), lengths))
    return result.transpose(1, 2, 0, 3)


def body(
    grid_field, send_blocks, donor_index, tile_choice, kernel_tiles, circle_len, slot_wave, legendre
):
    level_dev, band_blocks, lane_width = grid_field.shape
    send_count = send_blocks.shape[2]
    tile_count = kernel_tiles.shape[0]
    top_wave = legendre.shape[2]
    slot_per_device = legendre.shape[0]
    circ_band = band_blocks * lane_width // PTS
    band_index = lax.axis_index("lat")
    level_index = lax.axis_index("lev")
    level_groups = lax.axis_size("lev")
    outgoing = jnp.take(grid_field, send_blocks[0].reshape(-1), axis=1)
    widened_values = extended(outgoing, (("lat", 1),), send_count)
    donor_pool = jnp.concatenate(
        [grid_field, widened_values[:, :send_count], widened_values[:, 3 * send_count :]], axis=1
    )
    picked = jnp.take(donor_pool, donor_index.reshape(-1), axis=1).reshape(
        level_dev, band_blocks, 2, 1, lane_width
    )
    chosen = tile_choice[:, :, None] == jnp.arange(tile_count, dtype=jnp.int32)
    spread = jnp.where(chosen[None, :, :, :, None], picked, jnp.zeros((), jnp.bfloat16))
    spread = spread.reshape(level_dev * band_blocks, 2 * tile_count * lane_width)
    stacked = jnp.broadcast_to(kernel_tiles[None], (2, tile_count, lane_width, lane_width)).reshape(
        2 * tile_count * lane_width, lane_width
    )
    arrival = jnp.dot(spread, stacked, preferred_element_type=jnp.float32)
    squared = (arrival * arrival).astype(jnp.bfloat16).reshape(level_dev, circ_band, PTS)
    grouped = lax.all_to_all(squared, "lev", split_axis=1, concat_axis=0, tiled=True)
    circ_dev = circ_band // level_groups
    first_circle = band_index * circ_band + level_index * circ_dev
    lengths = lax.dynamic_slice_in_dim(circle_len, first_circle, circ_dev)
    coeffs = transform(grouped, lengths, slot_wave, top_wave)
    levels = coeffs.shape[0]
    slot_count = coeffs.shape[3]
    coeffs = coeffs.reshape(levels, 2, 1, 1, circ_dev, slot_count)
    arrived = lax.all_to_all(
        lax.all_to_all(coeffs, "lat", split_axis=5, concat_axis=2, tiled=True),
        "lev",
        split_axis=5,
        concat_axis=3,
        tiled=True,
    )
    gathered = arrived.reshape(levels, 2, -1, slot_per_device)
    spectra = jnp.einsum("lcgs,sgn->lcsn", gathered, legendre, preferred_element_type=jnp.float32)
    first_slot = (band_index * level_groups + level_index) * slot_per_device
    my_waves = lax.dynamic_slice_in_dim(slot_wave, first_slot, slot_per_device)
    allowed = jnp.arange(top_wave, dtype=jnp.int32)[None, :] >= my_waves[:, None]
    return jnp.where(allowed[None, None], spectra, 0.0).astype(jnp.bfloat16)


def solution(mesh):
    return jax.shard_map(
        body,
        mesh=mesh,
        in_specs=(
            P("lev", "lat", None),
            P("lat", None, None),
            P("lat", None),
            P("lat", None),
            P(),
            P(),
            P(),
            P(("lat", "lev"), None, None),
        ),
        out_specs=P(None, None, ("lat", "lev"), None),
        check_vma=False,
    )
```

profile of v0, /device:TPU:1, one launch (start us, length us, event | category | flops | bytes accessed | tf_op | source)
XLA Modules:
  0.0 218.9 jit_solution(17650958088679682755)
XLA Ops:
  1.4 2.2 %gather_fusion = bf16[256,2,128]{2,0,1:T(8,128)(2,1)S(1)} fusion(bf16[2,640,128]{2,1,0:T(8,128)(2,1)} %param.10, s32[1024]{0:T(1024)S(1)} %pad_clamp_fusion.1), kind=kCustom, calls=%fused_computation | custom fusion | bytes 263168 | tf_op jit(solution)/shard_map/jit(_take)/gather | solution.py:82
  3.8 4.8 %collective-permute-start = (bf16[2,128,128]{2,1,0:T(8,128)(2,1)S(1)}, bf16[2,128,128]{2,1,0:T(8,128)(2,1)S(1)}, u32[]{:S(2)}, u32[]{:S(2)}) collective-permute-start(bf16[2,128,128]{2,1,0:T(8,128)(2,1)S(1)} %get-tuple-element.122), channel_id=1, source_target_pairs={{0,16},{16,32},{32,48},{48,64},{64,80},{80,96},{96,112},{112,128},... | collective-permute-start | bytes 196616 | tf_op jit(solution)/shard_map/ppermute | solution.py:18
  15.0 4.4 %gather_fusion.1 = bf16[1280,2,128]{2,1,0:T(2,128)(2,1)S(1)} fusion(bf16[2,896,128]{2,0,1:T(2,128)(2,1)S(1)} %pad_maximum_fusion, s32[2048]{0:T(1024)S(1)} %pad_clamp_fusion), kind=kCustom, calls=%fused_computation.1 | custom fusion | bytes 1315840 | tf_op jit(solution)/shard_map/jit(_take)/gather | solution.py:87
  19.5 2.0 broadcast_select_fusion.1
  21.8 4.6 %broadcast_select_fusion = bf16[2,640,2,8,128]{4,3,2,1,0:T(8,128)(2,1)} fusion(pred[640,2,8]{2,1,0:T(4,128)(4,1)S(1)} %iota_compare_fusion.1, bf16[2,640,2,128]{3,2,1,0:T(2,128)(2,1)S(1)} %copy.31), kind=kLoop, calls=%fused_computation.41 | loop fusion | flops 2621440 | bytes 5908480 | tf_op jit(solution)/shard_map/jit(_where)/select_n | solution.py:91
  26.5 8.8 %select_n.130 = bf16[1280,2048]{1,0:T(8,128)(2,1)} reshape(bf16[2,640,2,8,128]{4,3,2,1,0:T(8,128)(2,1)} %broadcast_select_fusion) | data formatting | bytes 10485760 | tf_op jit(solution)/shard_map/jit(_where)/select_n | solution.py:91
  35.4 4.0 %fusion.41 = bf16[1280,128]{1,0:T(8,128)(2,1)S(1)} fusion(bf16[1280,2048]{1,0:T(8,128)(2,1)} %select_n.130, bf16[2048,128]{1,0:T(8,128)(2,1)S(1)} %bitcast.77), kind=kOutput, calls=%fused_computation.47 | convolution fusion | flops 671416320 | bytes 6094848 | tf_op jit(solution)/shard_map/dot_general | solution.py:96
  40.6 10.8 %all-to-all-start = ((bf16[2,16,5120]{2,0,1:T(2,128)(2,1)}), bf16[2,16,5120]{2,0,1:T(2,128)(2,1)S(1)}, u32[]{:S(2)}, u32[]{:S(2)}) async-start(bf16[2,16,5120]{2,0,1:T(2,128)(2,1)} %copy.32), calls=%async_computation | async-start | bytes 655360 | tf_op jit(solution)/shard_map/all_to_all | solution.py:98
  54.6 10.0 %all-to-all-done = bf16[2,16,5120]{2,0,1:T(2,128)(2,1)S(1)} async-done(((bf16[2,16,5120]{2,0,1:T(2,128)(2,1)}), bf16[2,16,5120]{2,0,1:T(2,128)(2,1)S(1)}, u32[]{:S(2)}, u32[]{:S(2)}) %all-to-all-start) | async-done | bytes 327712 | tf_op jit(solution)/shard_map/all_to_all | solution.py:98
  64.8 97.2 %while.19 = (s32[]{:T(128)}, bf16[12,32,256]{2,1,0:T(8,128)(2,1)S(1)}, s32[]{:T(128)}, s32[12,128]{1,0:T(8,128)}, s32[]{:T(128)}, /*index=5*/pred[]{:T(512)}, f32[]{:T(128)}, bf16[32,5120]{1,0:T(8,128)(2,1)S(1)}, s32[]{:T(128)}) while((s32[]{:T(128)}, bf16[12,32,256]{2,1,0:T(8,128)(2,1)S(1)}, s32[]{:T(128)}, s32[12,128]{1,0:T(8,128)}, ...), condition=%wide.region_1.2_spmd, body=%wide.region_0.1_spmd.sunk | while | flops 97222440 | bytes 11187395 | solution.py:59
  67.6 1.3 and_bitcast_fusion.2
  69.6 2.7 %fusion.63 = (bf16[5120,128]{1,0:T(8,128)(2,1)S(1)}, bf16[5120,128]{1,0:T(8,128)(2,1)S(1)}) fusion(bf16[40,128,128]{2,1,0:T(8,128)(2,1)S(1)} %get-tuple-element.185, pred[128]{0:T(512)(128)(4,1)S(1)} %and_bitcast_fusion.2, pred[5120]{0:T(1024)(128)(4,1)S(1)} %iota_compare_fusion.4, bf16[40,128,128]{2,1,0:T(8,128)(2,1)S(1)} %get-tuple-element.186), kind=kLoop, calls=%fused_computation.4.clone.1 | loop fusion | flops 1966080 | bytes 5248128 | tf_op jit(solution)/shard_map/convert
  75.7 1.3 and_bitcast_fusion.2
  77.7 2.7 %fusion.63 = (bf16[5120,128]{1,0:T(8,128)(2,1)S(1)}, bf16[5120,128]{1,0:T(8,128)(2,1)S(1)}) fusion(bf16[40,128,128]{2,1,0:T(8,128)(2,1)S(1)} %get-tuple-element.185, pred[128]{0:T(512)(128)(4,1)S(1)} %and_bitcast_fusion.2, pred[5120]{0:T(1024)(128)(4,1)S(1)} %iota_compare_fusion.4, bf16[40,128,128]{2,1,0:T(8,128)(2,1)S(1)} %get-tuple-element.186), kind=kLoop, calls=%fused_computation.4.clone.1 | loop fusion | flops 1966080 | bytes 5248128 | tf_op jit(solution)/shard_map/convert
  83.8 1.3 and_bitcast_fusion.2
  85.8 2.7 %fusion.63 = (bf16[5120,128]{1,0:T(8,128)(2,1)S(1)}, bf16[5120,128]{1,0:T(8,128)(2,1)S(1)}) fusion(bf16[40,128,128]{2,1,0:T(8,128)(2,1)S(1)} %get-tuple-element.185, pred[128]{0:T(512)(128)(4,1)S(1)} %and_bitcast_fusion.2, pred[5120]{0:T(1024)(128)(4,1)S(1)} %iota_compare_fusion.4, bf16[40,128,128]{2,1,0:T(8,128)(2,1)S(1)} %get-tuple-element.186), kind=kLoop, calls=%fused_computation.4.clone.1 | loop fusion | flops 1966080 | bytes 5248128 | tf_op jit(solution)/shard_map/convert
  93.9 2.7 %fusion.63 = (bf16[5120,128]{1,0:T(8,128)(2,1)S(1)}, bf16[5120,128]{1,0:T(8,128)(2,1)S(1)}) fusion(bf16[40,128,128]{2,1,0:T(8,128)(2,1)S(1)} %get-tuple-element.185, pred[128]{0:T(512)(128)(4,1)S(1)} %and_bitcast_fusion.2, pred[5120]{0:T(1024)(128)(4,1)S(1)} %iota_compare_fusion.4, bf16[40,128,128]{2,1,0:T(8,128)(2,1)S(1)} %get-tuple-element.186), kind=kLoop, calls=%fused_computation.4.clone.1 | loop fusion | flops 1966080 | bytes 5248128 | tf_op jit(solution)/shard_map/convert
  102.0 2.7 %fusion.63 = (bf16[5120,128]{1,0:T(8,128)(2,1)S(1)}, bf16[5120,128]{1,0:T(8,128)(2,1)S(1)}) fusion(bf16[40,128,128]{2,1,0:T(8,128)(2,1)S(1)} %get-tuple-element.185, pred[128]{0:T(512)(128)(4,1)S(1)} %and_bitcast_fusion.2, pred[5120]{0:T(1024)(128)(4,1)S(1)} %iota_compare_fusion.4, bf16[40,128,128]{2,1,0:T(8,128)(2,1)S(1)} %get-tuple-element.186), kind=kLoop, calls=%fused_computation.4.clone.1 | loop fusion | flops 1966080 | bytes 5248128 | tf_op jit(solution)/shard_map/convert
  110.1 2.7 %fusion.63 = (bf16[5120,128]{1,0:T(8,128)(2,1)S(1)}, bf16[5120,128]{1,0:T(8,128)(2,1)S(1)}) fusion(bf16[40,128,128]{2,1,0:T(8,128)(2,1)S(1)} %get-tuple-element.185, pred[128]{0:T(512)(128)(4,1)S(1)} %and_bitcast_fusion.2, pred[5120]{0:T(1024)(128)(4,1)S(1)} %iota_compare_fusion.4, bf16[40,128,128]{2,1,0:T(8,128)(2,1)S(1)} %get-tuple-element.186), kind=kLoop, calls=%fused_computation.4.clone.1 | loop fusion | flops 1966080 | bytes 5248128 | tf_op jit(solution)/shard_map/convert
  118.2 2.7 %fusion.63 = (bf16[5120,128]{1,0:T(8,128)(2,1)S(1)}, bf16[5120,128]{1,0:T(8,128)(2,1)S(1)}) fusion(bf16[40,128,128]{2,1,0:T(8,128)(2,1)S(1)} %get-tuple-element.185, pred[128]{0:T(512)(128)(4,1)S(1)} %and_bitcast_fusion.2, pred[5120]{0:T(1024)(128)(4,1)S(1)} %iota_compare_fusion.4, bf16[40,128,128]{2,1,0:T(8,128)(2,1)S(1)} %get-tuple-element.186), kind=kLoop, calls=%fused_computation.4.clone.1 | loop fusion | flops 1966080 | bytes 5248128 | tf_op jit(solution)/shard_map/convert
  126.3 2.7 %fusion.63 = (bf16[5120,128]{1,0:T(8,128)(2,1)S(1)}, bf16[5120,128]{1,0:T(8,128)(2,1)S(1)}) fusion(bf16[40,128,128]{2,1,0:T(8,128)(2,1)S(1)} %get-tuple-element.185, pred[128]{0:T(512)(128)(4,1)S(1)} %and_bitcast_fusion.2, pred[5120]{0:T(1024)(128)(4,1)S(1)} %iota_compare_fusion.4, bf16[40,128,128]{2,1,0:T(8,128)(2,1)S(1)} %get-tuple-element.186), kind=kLoop, calls=%fused_computation.4.clone.1 | loop fusion | flops 1966080 | bytes 5248128 | tf_op jit(solution)/shard_map/convert
  134.4 2.7 %fusion.63 = (bf16[5120,128]{1,0:T(8,128)(2,1)S(1)}, bf16[5120,128]{1,0:T(8,128)(2,1)S(1)}) fusion(bf16[40,128,128]{2,1,0:T(8,128)(2,1)S(1)} %get-tuple-element.185, pred[128]{0:T(512)(128)(4,1)S(1)} %and_bitcast_fusion.2, pred[5120]{0:T(1024)(128)(4,1)S(1)} %iota_compare_fusion.4, bf16[40,128,128]{2,1,0:T(8,128)(2,1)S(1)} %get-tuple-element.186), kind=kLoop, calls=%fused_computation.4.clone.1 | loop fusion | flops 1966080 | bytes 5248128 | tf_op jit(solution)/shard_map/convert
  142.5 2.7 %fusion.63 = (bf16[5120,128]{1,0:T(8,128)(2,1)S(1)}, bf16[5120,128]{1,0:T(8,128)(2,1)S(1)}) fusion(bf16[40,128,128]{2,1,0:T(8,128)(2,1)S(1)} %get-tuple-element.185, pred[128]{0:T(512)(128)(4,1)S(1)} %and_bitcast_fusion.2, pred[5120]{0:T(1024)(128)(4,1)S(1)} %iota_compare_fusion.4, bf16[40,128,128]{2,1,0:T(8,128)(2,1)S(1)} %get-tuple-element.186), kind=kLoop, calls=%fused_computation.4.clone.1 | loop fusion | flops 1966080 | bytes 5248128 | tf_op jit(solution)/shard_map/convert
  150.6 2.7 %fusion.63 = (bf16[5120,128]{1,0:T(8,128)(2,1)S(1)}, bf16[5120,128]{1,0:T(8,128)(2,1)S(1)}) fusion(bf16[40,128,128]{2,1,0:T(8,128)(2,1)S(1)} %get-tuple-element.185, pred[128]{0:T(512)(128)(4,1)S(1)} %and_bitcast_fusion.2, pred[5120]{0:T(1024)(128)(4,1)S(1)} %iota_compare_fusion.4, bf16[40,128,128]{2,1,0:T(8,128)(2,1)S(1)} %get-tuple-element.186), kind=kLoop, calls=%fused_computation.4.clone.1 | loop fusion | flops 1966080 | bytes 5248128 | tf_op jit(solution)/shard_map/convert
  158.7 2.7 %fusion.63 = (bf16[5120,128]{1,0:T(8,128)(2,1)S(1)}, bf16[5120,128]{1,0:T(8,128)(2,1)S(1)}) fusion(bf16[40,128,128]{2,1,0:T(8,128)(2,1)S(1)} %get-tuple-element.185, pred[128]{0:T(512)(128)(4,1)S(1)} %and_bitcast_fusion.2, pred[5120]{0:T(1024)(128)(4,1)S(1)} %iota_compare_fusion.4, bf16[40,128,128]{2,1,0:T(8,128)(2,1)S(1)} %get-tuple-element.186), kind=kLoop, calls=%fused_computation.4.clone.1 | loop fusion | flops 1966080 | bytes 5248128 | tf_op jit(solution)/shard_map/convert
  162.9 1.5 reshape.325
  164.4 15.8 %all-to-all-start.1 = ((bf16[48,2,1024]{2,1,0:T(2,128)(2,1)}), bf16[48,2,1024]{2,1,0:T(2,128)(2,1)S(1)}, u32[]{:S(2)}, u32[]{:S(2)}) async-start(bf16[48,2,1024]{2,1,0:T(2,128)(2,1)} %reshape.325), calls=%async_computation.1 | async-start | bytes 393216 | tf_op jit(solution)/shard_map/all_to_all | solution.py:107
  181.0 14.0 %all-to-all-done.1 = bf16[48,2,1024]{2,1,0:T(2,128)(2,1)S(1)} async-done(((bf16[48,2,1024]{2,1,0:T(2,128)(2,1)}), bf16[48,2,1024]{2,1,0:T(2,128)(2,1)S(1)}, u32[]{:S(2)}, u32[]{:S(2)}) %all-to-all-start.1) | async-done | bytes 196640 | tf_op jit(solution)/shard_map/all_to_all | solution.py:107
  196.6 1.5 reshape.327
  198.0 4.9 %all-to-all-start.2 = ((bf16[16,2,3072]{2,1,0:T(2,128)(2,1)}), bf16[16,2,3072]{2,1,0:T(2,128)(2,1)S(1)}, u32[]{:S(2)}, u32[]{:S(2)}) async-start(bf16[16,2,3072]{2,1,0:T(2,128)(2,1)} %reshape.327), calls=%async_computation.2 | async-start | bytes 393216 | tf_op jit(solution)/shard_map/all_to_all | solution.py:106
  203.0 10.2 %all-to-all-done.2 = bf16[16,2,3072]{2,1,0:T(2,128)(2,1)S(1)} async-done(((bf16[16,2,3072]{2,1,0:T(2,128)(2,1)}), bf16[16,2,3072]{2,1,0:T(2,128)(2,1)S(1)}, u32[]{:S(2)}, u32[]{:S(2)}) %all-to-all-start.2) | async-done | bytes 196640 | tf_op jit(solution)/shard_map/all_to_all | solution.py:106
  214.9 2.9 %fusion.42 = bf16[32,2,2,1280]{3,0,1,2:T(8,128)(2,1)S(1)} fusion(bf16[2,768,1280]{2,1,0:T(8,128)(2,1)} %param.17, bf16[32,2,768,2]{0,3,2,1:T(2,128)(2,1)S(1)} %bitcast.69, pred[2,1280]{1,0:T(4,128)(4,1)S(1)} %iota_compare_fusion.2), kind=kOutput, calls=%fused_computation.48 | convolution fusion | flops 251985920 | bytes 4459008 | tf_op jit(solution)/shard_map/lcgs,sgn->lcsn/dot_general | solution.py:114
  (136 shorter events, 77.4 us)
Async XLA Ops:
  0.0 35.3 %copy-start = (bf16[8,128,128]{2,1,0:T(8,128)(2,1)S(1)}, bf16[8,128,128]{2,1,0:T(8,128)(2,1)}, u32[]{:S(2)}) copy-start(bf16[8,128,128]{2,1,0:T(8,128)(2,1)} %param.14) | copy-start | bytes 786436
  0.0 12.1 %copy-start.1 = (s32[640,2]{0,1:T(2,128)S(1)}, s32[640,2]{0,1:T(2,128)}, u32[]{:S(2)}) copy-start(s32[640,2]{0,1:T(2,128)} %param.12) | copy-start | bytes 15364
  0.0 12.6 %copy-start.2 = (s32[640,2]{0,1:T(2,128)S(1)}, s32[640,2]{0,1:T(2,128)}, u32[]{:S(2)}) copy-start(s32[640,2]{0,1:T(2,128)} %param.13) | copy-start | bytes 15364
  3.8 10.0 %collective-permute-start = (bf16[2,128,128]{2,1,0:T(8,128)(2,1)S(1)}, bf16[2,128,128]{2,1,0:T(8,128)(2,1)S(1)}, u32[]{:S(2)}, u32[]{:S(2)}) collective-permute-start(bf16[2,128,128]{2,1,0:T(8,128)(2,1)S(1)} %get-tuple-element.122), channel_id=1, source_target_pairs={{0,16},{16,32},{32,48},{48,64},{64,80},{80,96},{96,112},{112,128},... | collective-permute-start | bytes 196616 | tf_op jit(solution)/shard_map/ppermute | solution.py:18
  8.6 5.6 %collective-permute-start.1 = (bf16[2,128,128]{2,1,0:T(8,128)(2,1)S(1)}, bf16[2,128,128]{2,1,0:T(8,128)(2,1)S(1)}, u32[]{:S(2)}, u32[]{:S(2)}) collective-permute-start(bf16[2,128,128]{2,1,0:T(8,128)(2,1)S(1)} %get-tuple-element.123), channel_id=1, source_target_pairs={{16,0},{32,16},{48,32},{64,48},{80,64},{96,80},{112,96},{128,112},... | collective-permute-start | bytes 196616 | tf_op jit(solution)/shard_map/ppermute | solution.py:19
  40.6 24.1 %all-to-all-start = ((bf16[2,16,5120]{2,0,1:T(2,128)(2,1)}), bf16[2,16,5120]{2,0,1:T(2,128)(2,1)S(1)}, u32[]{:S(2)}, u32[]{:S(2)}) async-start(bf16[2,16,5120]{2,0,1:T(2,128)(2,1)} %copy.32), calls=%async_computation | async-start | bytes 655360 | tf_op jit(solution)/shard_map/all_to_all | solution.py:98
  164.4 30.6 %all-to-all-start.1 = ((bf16[48,2,1024]{2,1,0:T(2,128)(2,1)}), bf16[48,2,1024]{2,1,0:T(2,128)(2,1)S(1)}, u32[]{:S(2)}, u32[]{:S(2)}) async-start(bf16[48,2,1024]{2,1,0:T(2,128)(2,1)} %reshape.325), calls=%async_computation.1 | async-start | bytes 393216 | tf_op jit(solution)/shard_map/all_to_all | solution.py:107
  198.0 15.2 %all-to-all-start.2 = ((bf16[16,2,3072]{2,1,0:T(2,128)(2,1)}), bf16[16,2,3072]{2,1,0:T(2,128)(2,1)S(1)}, u32[]{:S(2)}, u32[]{:S(2)}) async-start(bf16[16,2,3072]{2,1,0:T(2,128)(2,1)} %reshape.327), calls=%async_computation.2 | async-start | bytes 393216 | tf_op jit(solution)/shard_map/all_to_all | solution.py:106
where the time goes:
time: 221 us; the launch traced here: 219 us
  other arithmetic  91.6 us (41%)
  local copies, waits for them, and re-layouts  38.9 us (18%)
  starting transfers between devices  37.6 us (17%)
  waiting for transfers between devices  34.6 us (16%)
  matrix products  13.6 us (6%)
  between operations  2.22 us (1%)
    another operation x13, other arithmetic  32.4 us
    and x12, other arithmetic, circle_table(): (jnp.arange(points, dtype=jnp.int32) < length)[:, None] & live_slot[None, :]  15.9 us
    all_to_all x1, starting transfers between devices, body(): lax.all_to_all(coeffs, 'lat', split_axis=5, concat_axis=2, tiled=True)  15.8 us
    all_to_all x1, waiting for transfers between devices, body(): lax.all_to_all(coeffs, 'lat', split_axis=5, concat_axis=2, tiled=True)  14 us
    cos x12, other arithmetic, circle_table(): cos_lo = jnp.cos(lower_angle)[None]  11 us
    all_to_all x1, starting transfers between devices, body(): lax.all_to_all(squared, 'lev', split_axis=1, concat_axis=0, tiled=True)  10.8 us
    all_to_all x1, waiting for transfers between devices, body(): lax.all_to_all(lax.all_to_all(coeffs, 'lat', split_axis=5, concat_axis=2,...  10.2 us
    all_to_all x1, waiting for transfers between devices, body(): lax.all_to_all(squared, 'lev', split_axis=1, concat_axis=0, tiled=True)  10 us
  transfers between devices with their start and end apart: 5, of which 4 were waited for; matrix products, arithmetic and copies ran while one was open for 3% of the time, Pallas kernels for 0%

commit v1 on v0

v1 whole, which is shorter than its diff:
```python
import functools

import jax
import jax.numpy as jnp
from jax import lax
from jax.experimental import pallas as pl
from jax.experimental.pallas import tpu as pltpu
from jax.sharding import PartitionSpec as P

PTS = 5120
FINE = 128
CHUNK = 256

SIN_COEF = (3.1415927410125732, -5.167709827423096, 2.550076961517334, -0.5982874631881714, 0.07764891535043716)
COS_COEF = (1.0, -4.934792518615723, 4.058409690856934, -1.331863284111023, 0.21965928375720978)


def poly(coef, x):
    acc = jnp.full_like(x, coef[-1])
    for c in coef[-2::-1]:
        acc = acc * x + c
    return acc


def phase(steps, length, inverse):
    turns = jnp.floor(steps * inverse + 0.5)
    u = (steps - turns * length) * inverse
    u2 = u * u
    s = u * poly(SIN_COEF, u2)
    c = poly(COS_COEF, u2)
    return 1.0 - 2.0 * s * s, -2.0 * s * c


def times(a, b):
    return a[0] * b[0] - a[1] * b[1], a[0] * b[1] + a[1] * b[0]


def local_kernel(
    top_wave, grid_ref, below_ref, above_ref, donor_ref, tile_ref, kern_ref, len_ref, wave_ref,
    out_ref, pool_scr, diag_scr, idx_scr, x_scr, len_scr, coef_scr
):
    levels, blocks, lanes = grid_ref.shape
    cap = below_ref.shape[1]
    pool_size = blocks + 2 * cap
    tiles = kern_ref.shape[0]
    circles = x_scr.shape[0]
    per_circle = blocks // circles
    width = levels * lanes
    band = lax.axis_index("lat")

    for l in range(levels):
        cols = slice(l * lanes, (l + 1) * lanes)
        pool_scr[0:blocks, cols] = grid_ref[l]
        pool_scr[blocks : blocks + cap, cols] = below_ref[l]
        pool_scr[blocks + cap : pool_size, cols] = above_ref[l]
    diag_scr[...] = jnp.zeros_like(diag_scr)
    for t in range(tiles):
        for l in range(levels):
            cols = slice(l * lanes, (l + 1) * lanes)
            diag_scr[t, cols, cols] = kern_ref[t]
    idx_scr[...] = jnp.zeros_like(idx_scr)
    idx_scr[0:2, :] = donor_ref[...].astype(jnp.float32)
    idx_scr[2:4, :] = tile_ref[...].astype(jnp.float32)
    columns = idx_scr[...].T

    group = 4
    rows = group * per_circle
    for start in range(0, circles, group):
        part = columns[start * per_circle : (start + group) * per_circle, :]
        total = jnp.zeros((rows, width), jnp.float32)
        spots = lax.broadcasted_iota(jnp.int32, (rows, pool_size), 1).astype(jnp.float32)
        for k in range(2):
            hot = jnp.where(spots == part[:, k : k + 1], 1.0, 0.0).astype(jnp.bfloat16)
            picked = jnp.dot(hot, pool_scr[...], preferred_element_type=jnp.float32)
            which = part[:, 2 + k : 3 + k]
            for t in range(tiles):
                chosen = jnp.where(which == float(t), picked, 0.0).astype(jnp.bfloat16)
                total += jnp.dot(chosen, diag_scr[t], preferred_element_type=jnp.float32)
        squared = total * total
        for c in range(group):
            n = len_ref[band * circles + start + c]
            spot = lax.broadcasted_iota(jnp.int32, (per_circle, lanes), 0) * lanes
            spot = spot + lax.broadcasted_iota(jnp.int32, (per_circle, lanes), 1)
            for l in range(levels):
                piece = squared[c * per_circle : (c + 1) * per_circle, l * lanes : (l + 1) * lanes]
                piece = jnp.where(spot < n, piece, 0.0).astype(jnp.bfloat16)
                x_scr[start + c, 48 * l : 48 * l + per_circle, :] = piece
            len_scr[start + c : start + c + 1, :] = jnp.full((1, CHUNK), n, jnp.int32).astype(jnp.float32)

    slots = wave_ref.shape[1]
    row = lax.broadcasted_iota(jnp.int32, (8, CHUNK), 0).astype(jnp.float32)
    for chunk in range(slots // CHUNK):
        span = slice(chunk * CHUNK, (chunk + 1) * CHUNK)
        wave = wave_ref[:, span]
        wave_rows = row * wave

        def circle(g, carry):
            length = len_scr[pl.ds(g, 1), :]
            inverse = 1.0 / length
            base = phase(wave_rows, length, inverse)
            outer = phase(wave_rows * float(FINE), length, inverse)
            step = times((base[0][7:8], base[1][7:8]), (base[0][1:2], base[1][1:2]))
            jump = times((outer[0][7:8], outer[1][7:8]), (outer[0][1:2], outer[1][1:2]))
            twice = jnp.broadcast_to(2.0 * step[0], base[0].shape)
            second = times(base, step)
            cos_rows, sin_rows = [base[0], second[0]], [base[1], second[1]]
            for q in range(2, FINE // 8):
                cos_rows.append(twice * cos_rows[-1] - cos_rows[-2])
                sin_rows.append(twice * sin_rows[-1] - sin_rows[-2])
            cos_table = jnp.concatenate(cos_rows, axis=0).astype(jnp.bfloat16)
            sin_table = jnp.concatenate(sin_rows, axis=0).astype(jnp.bfloat16)
            x = x_scr[g]
            real = jnp.dot(x, cos_table, preferred_element_type=jnp.float32)
            imag = jnp.dot(x, sin_table, preferred_element_type=jnp.float32)
            jump = (jnp.broadcast_to(jump[0], row.shape), jnp.broadcast_to(jump[1], row.shape))
            live = (wave >= 1.0) & (wave < float(top_wave)) & (2.0 * wave < length)
            for l in range(levels):
                last = per_circle // 8 - 1
                at = 48 * l + 8 * last
                total = (real[at : at + 8], imag[at : at + 8])
                for q in range(last - 1, -1, -1):
                    at = 48 * l + 8 * q
                    turned = times(total, jump)
                    total = (turned[0] + real[at : at + 8], turned[1] + imag[at : at + 8])
                total = times(total, outer)
                for c in range(2):
                    value = jnp.sum(total[c], axis=0, keepdims=True)
                    coef_scr[2 * l + c, pl.ds(g, 1), span] = jnp.where(live, value, 0.0)
            return carry

        lax.fori_loop(0, circles, circle, 0)

    quarter = lax.broadcasted_iota(jnp.int32, (circles, 128), 1) // 32
    for block in range(slots // 128):
        parts = [coef_scr[k, :, block * 128 : (block + 1) * 128] for k in range(4)]
        for to in range(4):
            value = parts[to]
            for k in range(4):
                if k != to:
                    value = jnp.where(quarter == k, pltpu.roll(parts[k], (32 * (k - to)) % 128, 1), value)
            out_ref[block * 4 + to] = value.astype(jnp.bfloat16)


def transform_band(grid, below, above, donor, choice, kernels, lengths, waves, bands, top_wave):
    levels, blocks, lanes = grid.shape
    circles = blocks * lanes // PTS
    slots = waves.shape[1]
    vmem = pl.BlockSpec(memory_space=pltpu.VMEM)
    return pl.pallas_call(
        functools.partial(local_kernel, top_wave),
        out_shape=jax.ShapeDtypeStruct((bands, circles, 128), jnp.bfloat16),
        in_specs=[vmem] * 6 + [pl.BlockSpec(memory_space=pltpu.SMEM), vmem],
        out_specs=vmem,
        scratch_shapes=[
            pltpu.VMEM((blocks + 2 * below.shape[1], levels * lanes), jnp.bfloat16),
            pltpu.VMEM((kernels.shape[0], levels * lanes, levels * lanes), jnp.bfloat16),
            pltpu.VMEM((8, blocks), jnp.float32),
            pltpu.VMEM((circles, 96, lanes), jnp.bfloat16),
            pltpu.VMEM((circles, CHUNK), jnp.float32),
            pltpu.VMEM((4, circles, slots), jnp.float32),
        ],
        compiler_params=pltpu.CompilerParams(vmem_limit_bytes=48 * 1024 * 1024),
        name="interpolate_and_transform",
    )(grid, below, above, donor, choice, kernels, lengths, waves)


def shift_bands(outgoing, cap):
    size = lax.axis_size("lat")
    up = [(i, i + 1) for i in range(size - 1)]
    down = [(j, i) for i, j in up]
    below = lax.ppermute(outgoing[:, cap:], "lat", up)
    above = lax.ppermute(outgoing[:, :cap], "lat", down)
    return below, above


def body(
    grid_field, send_blocks, donor_index, tile_choice, kernel_tiles, circle_len, slot_wave, legendre
):
    levels, blocks, lanes = grid_field.shape
    cap = send_blocks.shape[2]
    top_wave = legendre.shape[2]
    slot_dev = legendre.shape[0]
    circles = blocks * lanes // PTS
    bands = lax.axis_size("lat")
    level_groups = lax.axis_size("lev")
    slots = slot_wave.shape[0]
    outgoing = jnp.take(grid_field, send_blocks[0].reshape(-1), axis=1)
    below, above = shift_bands(outgoing, cap)
    tiles_out = transform_band(
        grid_field, below, above, donor_index.T, tile_choice.T, kernel_tiles, circle_len,
        slot_wave.astype(jnp.float32).reshape(1, slots), bands, top_wave,
    )
    arrived = lax.all_to_all(tiles_out, "lat", split_axis=0, concat_axis=0, tiled=True)
    arrived = arrived.reshape(bands * circles, 4, level_groups, slot_dev)
    turned = arrived.transpose(2, 1, 3, 0).reshape(level_groups, 4 * slot_dev, bands * circles)
    gathered = lax.all_to_all(turned, "lev", split_axis=0, concat_axis=0, tiled=True)
    gathered = gathered.reshape(level_groups * 4, slot_dev, bands * circles)
    spectra = jnp.einsum("rsg,sgn->rsn", gathered, legendre, preferred_element_type=jnp.float32)
    first = (lax.axis_index("lat") * level_groups + lax.axis_index("lev")) * slot_dev
    mine = lax.dynamic_slice_in_dim(slot_wave, first, slot_dev)
    allowed = jnp.arange(top_wave, dtype=jnp.int32)[None, :] >= mine[:, None]
    spectra = jnp.where(allowed[None], spectra, 0.0).astype(jnp.bfloat16)
    return spectra.reshape(level_groups * levels, 2, slot_dev, top_wave)


def solution(mesh):
    return jax.shard_map(
        body,
        mesh=mesh,
        in_specs=(
            P("lev", "lat", None),
            P("lat", None, None),
            P("lat", None),
            P("lat", None),
            P(),
            P(),
            P(),
            P(("lat", "lev"), None, None),
        ),
        out_specs=P(None, None, ("lat", "lev"), None),
        check_vma=False,
    )
```

time: 221 us -> 105 us (0.48)
  other arithmetic: 91.6 us -> 2.25 us
  Pallas kernels: 0 us -> 28 us
  local copies, waits for them, and re-layouts: 38.9 us -> 11.1 us
  waiting for transfers between devices: 34.6 us -> 22.8 us
  matrix products: 13.6 us -> 2.89 us
    another operation x13 -> x0, other arithmetic: 32.4 us -> none
    pallas_call x0 -> x1, Pallas kernels: none -> 28 us  [transform_band(): pl.pallas_call(functools.partial(local_kernel, top_wave), out_shape=jax.S...]
    and x13 -> x0, other arithmetic: 16 us -> none  [the longest x12 15.9 us: circle_table(): (jnp.arange(points, dtype=jnp.int32) < length)[:, None] & live_slot[None, :]]
    cos x24 -> x0, other arithmetic: 16 us -> none  [the longest x12 11 us: circle_table(): cos_lo = jnp.cos(lower_angle)[None]]
    all_to_all x3 -> x2, waiting for transfers between devices: 34.2 us -> 22.2 us  [the longest x1 12.1 us: body(): lax.all_to_all(tiles_out, 'lat', split_axis=0, concat_axis=0, tiled=True)]
    dot_general x14 -> x1, matrix products: 13.6 us -> 2.89 us  [body(): jnp.einsum('rsg,sgn->rsn', gathered, legendre, preferred_element_type=jnp...]
    sub x12 -> x0, other arithmetic: 9.73 us -> none  [circle_table(): cosine = (cos_hi * cos_lo - sin_hi * sin_lo).reshape(points, -1)]
    select_n x2 -> x0, local copies, waits for them, and re-layouts: 9.14 us -> none  [the longest x1 8.8 us: body(): jnp.where(chosen[None, :, :, :, None], picked, jnp.zeros((), jnp.bfloat16))]
  transfers between devices with their start and end apart: 5 -> 4, of which waited for: 4 -> 3; matrix products, arithmetic and copies ran while one was open for 3% -> 1% of each run, Pallas kernels for 0% -> 0%
where the time goes in v1:
time: 105 us; the launch traced here: 104 us
  starting transfers between devices  37.2 us (35%)
  Pallas kernels  28 us (27%)
  waiting for transfers between devices  22.8 us (22%)
  local copies, waits for them, and re-layouts  11.1 us (11%)
  matrix products  2.89 us (3%)
  other arithmetic  2.25 us (2%)
    pallas_call x1, Pallas kernels, transform_band(): pl.pallas_call(functools.partial(local_kernel, top_wave), out_shape=jax.S...  28 us
    all_to_all x1, starting transfers between devices, body(): lax.all_to_all(tiles_out, 'lat', split_axis=0, concat_axis=0, tiled=True)  19.2 us
    all_to_all x1, waiting for transfers between devices, body(): lax.all_to_all(tiles_out, 'lat', split_axis=0, concat_axis=0, tiled=True)  12.1 us
    all_to_all x1, starting transfers between devices, body(): lax.all_to_all(turned, 'lev', split_axis=0, concat_axis=0, tiled=True)  11.3 us
    all_to_all x1, waiting for transfers between devices, body(): lax.all_to_all(turned, 'lev', split_axis=0, concat_axis=0, tiled=True)  10.1 us
    ppermute x1, starting transfers between devices, shift_bands(): below = lax.ppermute(outgoing[:, cap:], 'lat', up)  5.45 us
    unnamed x10, local copies, waits for them, and re-layouts  3.99 us
    dot_general x1, matrix products, body(): jnp.einsum('rsg,sgn->rsn', gathered, legendre, preferred_element_type=jnp...  2.89 us
  transfers between devices with their start and end apart: 4, of which 3 were waited for; matrix products, arithmetic and copies ran while one was open for 1% of the time, Pallas kernels for 0%

profile of v1, /device:TPU:1, one launch (start us, length us, event | category | flops | bytes accessed | tf_op | source)
XLA Modules:
  0.0 104.4 jit_solution(350976784508517296)
XLA Ops:
  0.0 0.7 compare_and_fusion
  0.7 0.7 compare_select_fusion
  1.4 2.2 %gather_fusion = bf16[256,2,128]{2,0,1:T(8,128)(2,1)S(1)} fusion(bf16[2,640,128]{2,1,0:T(8,128)(2,1)} %grid_ref.1, s32[1024]{0:T(1024)S(1)} %pad_clamp_fusion), kind=kCustom, calls=%fused_computation | custom fusion | bytes 263168 | tf_op jit(solution)/shard_map/jit(_take)/gather | solution.py:187
  3.6 0.1 select_bitcast_fusion
  3.8 1.3 %collective-permute-start.1 = (bf16[2,128,128]{2,1,0:T(8,128)(2,1)S(1)}, bf16[2,128,128]{2,1,0:T(8,128)(2,1)S(1)}, u32[]{:S(2)}, u32[]{:S(2)}) collective-permute-start(bf16[2,128,128]{2,1,0:T(8,128)(2,1)S(1)} %get-tuple-element.5), channel_id=1, source_target_pairs={{16,0},{32,16},{48,32},{64,48},{80,64},{96,80},{112,96},{128,112},... | collective-permute-start | bytes 196616 | tf_op jit(solution)/shard_map/ppermute | solution.py:172
  5.1 5.4 %collective-permute-start = (bf16[2,128,128]{2,1,0:T(8,128)(2,1)S(1)}, bf16[2,128,128]{2,1,0:T(8,128)(2,1)S(1)}, u32[]{:S(2)}, u32[]{:S(2)}) collective-permute-start(bf16[2,128,128]{2,1,0:T(8,128)(2,1)S(1)} %get-tuple-element.6), channel_id=1, source_target_pairs={{0,16},{16,32},{32,48},{48,64},{64,80},{80,96},{96,112},{112,128},... | collective-permute-start | bytes 196616 | tf_op jit(solution)/shard_map/ppermute | solution.py:171
  10.5 0.7 convert_element_type.9
  11.2 0.0 collective-permute-done.1.above_ref
  11.2 0.6 collective-permute-done.below_ref
  11.8 0.0 copy-start
  11.8 1.0 copy-done
  12.8 0.0 copy-start.1
  12.8 0.9 copy-done.1
  13.7 0.0 copy-start.2
  13.7 0.7 copy-done.2
  14.4 0.0 copy-start.3
  14.4 0.7 copy-done.3
  15.1 0.0 copy-start.4
  15.1 0.7 copy-done.4
  15.8 28.0 %interpolate_and_transform.1 = bf16[48,16,128]{2,1,0:T(8,128)(2,1)} custom-call(bf16[2,640,128]{2,1,0:T(8,128)(2,1)S(1)} %copy-done, bf16[2,128,128]{2,1,0:T(8,128)(2,1)S(1)} %collective-permute-done.below_ref, bf16[2,128,128]{2,1,0:T(8,128)(2,1)S(1)} %collective-permute-done.1.above_ref, s32[2,640]{1,0:T(2,128)S(1)} %bitcast.16, s32[2,640]{1,0:T(2,128)S(1)} %bitcast.17, ...), custom_call_target="tpu_custom_call" | custom-call | tf_op jit(solution)/shard_map/interpolate_and_transform/pallas_call | solution.py:149
  43.8 19.2 %all-to-all-start = ((bf16[48,16,128]{2,1,0:T(8,128)(2,1)}), bf16[48,16,128]{2,1,0:T(8,128)(2,1)S(1)}, u32[]{:S(2)}, u32[]{:S(2)}) async-start(bf16[48,16,128]{2,1,0:T(8,128)(2,1)} %interpolate_and_transform.1), calls=%async_computation | async-start | bytes 393216 | tf_op jit(solution)/shard_map/all_to_all | solution.py:193
  63.0 0.8 dynamic_slice.3
  63.8 12.1 %all-to-all-done = bf16[48,16,128]{2,1,0:T(8,128)(2,1)S(1)} async-done(((bf16[48,16,128]{2,1,0:T(8,128)(2,1)}), bf16[48,16,128]{2,1,0:T(8,128)(2,1)S(1)}, u32[]{:S(2)}, u32[]{:S(2)}) %all-to-all-start) | async-done | bytes 196640 | tf_op jit(solution)/shard_map/all_to_all | solution.py:193
  75.9 0.9 copy.15
  76.8 1.2 %reshape.68 = bf16[768,4,16,2]{0,3,2,1:T(2,128)(2,1)S(1)} reshape(bf16[48,16,128]{1,0,2:T(8,128)(2,1)S(1)} %copy.15) | data formatting | bytes 393216 | tf_op jit(solution)/shard_map/reshape | solution.py:194
  78.1 0.7 copy.17
  78.8 11.3 %all-to-all-start.1 = ((bf16[16,8,768]{2,1,0:T(8,128)(2,1)}), bf16[16,8,768]{2,1,0:T(8,128)(2,1)S(1)}, u32[]{:S(2)}, u32[]{:S(2)}) async-start(bf16[16,8,768]{2,1,0:T(8,128)(2,1)} %copy.17), calls=%async_computation.1 | async-start | bytes 393216 | tf_op jit(solution)/shard_map/all_to_all | solution.py:196
  90.1 0.1 iota_compare_fusion
  90.2 10.1 %all-to-all-done.1 = bf16[16,8,768]{2,1,0:T(8,128)(2,1)S(1)} async-done(((bf16[16,8,768]{2,1,0:T(8,128)(2,1)}), bf16[16,8,768]{2,1,0:T(8,128)(2,1)S(1)}, u32[]{:S(2)}, u32[]{:S(2)}) %all-to-all-start.1) | async-done | bytes 196640 | tf_op jit(solution)/shard_map/all_to_all | solution.py:196
  100.3 0.1 reshape.70
  100.4 2.9 %fusion.1 = bf16[64,2,1280]{2,0,1:T(8,128)(2,1)S(1)} fusion(bf16[2,768,1280]{2,1,0:T(8,128)(2,1)} %param.15, pred[2,1280]{1,0:T(4,128)(4,1)S(1)} %iota_compare_fusion, bf16[64,2,768]{2,1,0:T(2,128)(2,1)S(1)} %reshape.70), kind=kOutput, calls=%fused_computation.3 | convolution fusion | flops 251985920 | bytes 4459008 | tf_op jit(solution)/shard_map/rsg,sgn->rsn/dot_general | solution.py:198
  103.3 1.1 %copy.20 = bf16[64,2,1280]{2,1,0:T(2,128)(2,1)} copy(bf16[64,2,1280]{2,0,1:T(8,128)(2,1)S(1)} %fusion.1) | data formatting | bytes 655360 | tf_op jit(solution)/shard_map/reshape | solution.py:203
  (4 shorter events, 0.1 us)
Async XLA Ops:
  3.8 7.5 %collective-permute-start.1 = (bf16[2,128,128]{2,1,0:T(8,128)(2,1)S(1)}, bf16[2,128,128]{2,1,0:T(8,128)(2,1)S(1)}, u32[]{:S(2)}, u32[]{:S(2)}) collective-permute-start(bf16[2,128,128]{2,1,0:T(8,128)(2,1)S(1)} %get-tuple-element.5), channel_id=1, source_target_pairs={{16,0},{32,16},{48,32},{64,48},{80,64},{96,80},{112,96},{128,112},... | collective-permute-start | bytes 196616 | tf_op jit(solution)/shard_map/ppermute | solution.py:172
  5.1 6.8 %collective-permute-start = (bf16[2,128,128]{2,1,0:T(8,128)(2,1)S(1)}, bf16[2,128,128]{2,1,0:T(8,128)(2,1)S(1)}, u32[]{:S(2)}, u32[]{:S(2)}) collective-permute-start(bf16[2,128,128]{2,1,0:T(8,128)(2,1)S(1)} %get-tuple-element.6), channel_id=1, source_target_pairs={{0,16},{16,32},{32,48},{48,64},{64,80},{80,96},{96,112},{112,128},... | collective-permute-start | bytes 196616 | tf_op jit(solution)/shard_map/ppermute | solution.py:171
  11.8 1.0 copy-start
  12.8 0.9 copy-start.1
  13.7 0.7 copy-start.2
  14.4 0.7 copy-start.3
  15.1 0.7 copy-start.4
  43.8 32.1 %all-to-all-start = ((bf16[48,16,128]{2,1,0:T(8,128)(2,1)}), bf16[48,16,128]{2,1,0:T(8,128)(2,1)S(1)}, u32[]{:S(2)}, u32[]{:S(2)}) async-start(bf16[48,16,128]{2,1,0:T(8,128)(2,1)} %interpolate_and_transform.1), calls=%async_computation | async-start | bytes 393216 | tf_op jit(solution)/shard_map/all_to_all | solution.py:193
  78.8 21.5 %all-to-all-start.1 = ((bf16[16,8,768]{2,1,0:T(8,128)(2,1)}), bf16[16,8,768]{2,1,0:T(8,128)(2,1)S(1)}, u32[]{:S(2)}, u32[]{:S(2)}) async-start(bf16[16,8,768]{2,1,0:T(8,128)(2,1)} %copy.17), calls=%async_computation.1 | async-start | bytes 393216 | tf_op jit(solution)/shard_map/all_to_all | solution.py:196

commit v2 on v1

v2 whole, which is shorter than its diff:
```python
import functools

import jax
import jax.numpy as jnp
from jax import lax
from jax.experimental import pallas as pl
from jax.experimental.pallas import tpu as pltpu
from jax.sharding import PartitionSpec as P

PTS = 5120
FINE = 128
CHUNK = 256
PAIR = 2

SIN_COEF = (3.1415927410125732, -5.167709827423096, 2.550076961517334, -0.5982874631881714, 0.07764891535043716)
COS_COEF = (1.0, -4.934792518615723, 4.058409690856934, -1.331863284111023, 0.21965928375720978)


def poly(coef, x):
    acc = jnp.full_like(x, coef[-1])
    for c in coef[-2::-1]:
        acc = acc * x + c
    return acc


def phase(steps, length, inverse):
    turns = jnp.floor(steps * inverse + 0.5)
    u = (steps - turns * length) * inverse
    u2 = u * u
    s = u * poly(SIN_COEF, u2)
    c = poly(COS_COEF, u2)
    return 1.0 - 2.0 * s * s, -2.0 * s * c


def times(a, b):
    return a[0] * b[0] - a[1] * b[1], a[0] * b[1] + a[1] * b[0]


MESH = pl.DeviceIdType.MESH


def fill_donors(grid_ref, below_ref, above_ref, donor_ref, tile_ref, kern_ref, pool_scr, diag_scr, idx_scr):
    levels, blocks, lanes = grid_ref.shape
    cap = below_ref.shape[1]
    for l in range(levels):
        cols = slice(l * lanes, (l + 1) * lanes)
        pool_scr[0:blocks, cols] = grid_ref[l]
        pool_scr[blocks : blocks + cap, cols] = below_ref[l]
        pool_scr[blocks + cap : blocks + 2 * cap, cols] = above_ref[l]
    diag_scr[...] = jnp.zeros_like(diag_scr)
    for t in range(kern_ref.shape[0]):
        for l in range(levels):
            cols = slice(l * lanes, (l + 1) * lanes)
            diag_scr[t, cols, cols] = kern_ref[t]
    idx_scr[...] = jnp.zeros_like(idx_scr)
    idx_scr[0:2, :] = donor_ref[...].astype(jnp.float32)
    idx_scr[2:4, :] = tile_ref[...].astype(jnp.float32)


def interpolate(band, len_ref, pool_scr, diag_scr, idx_scr, x_scr, len_scr):
    pool_size, width = pool_scr.shape
    tiles = diag_scr.shape[0]
    circles, _, lanes = x_scr.shape
    levels = width // lanes
    per_circle = idx_scr.shape[1] // circles
    columns = idx_scr[...].T
    group = 4
    rows = group * per_circle
    for start in range(0, circles, group):
        part = columns[start * per_circle : (start + group) * per_circle, :]
        total = jnp.zeros((rows, width), jnp.float32)
        spots = lax.broadcasted_iota(jnp.int32, (rows, pool_size), 1).astype(jnp.float32)
        for k in range(2):
            hot = jnp.where(spots == part[:, k : k + 1], 1.0, 0.0).astype(jnp.bfloat16)
            picked = jnp.dot(hot, pool_scr[...], preferred_element_type=jnp.float32)
            which = part[:, 2 + k : 3 + k]
            for t in range(tiles):
                chosen = jnp.where(which == float(t), picked, 0.0).astype(jnp.bfloat16)
                total += jnp.dot(chosen, diag_scr[t], preferred_element_type=jnp.float32)
        squared = total * total
        for c in range(group):
            n = len_ref[band * circles + start + c]
            spot = lax.broadcasted_iota(jnp.int32, (per_circle, lanes), 0) * lanes
            spot = spot + lax.broadcasted_iota(jnp.int32, (per_circle, lanes), 1)
            for l in range(levels):
                piece = squared[c * per_circle : (c + 1) * per_circle, l * lanes : (l + 1) * lanes]
                piece = jnp.where(spot < n, piece, 0.0).astype(jnp.bfloat16)
                x_scr[start + c, 48 * l : 48 * l + per_circle, :] = piece
            len_scr[start + c : start + c + 1, :] = jnp.full((1, CHUNK), n, jnp.int32).astype(jnp.float32)


def transform_circle(g, wave, top_wave, levels, per_circle, x_scr, len_scr, coef_scr):
    row = lax.broadcasted_iota(jnp.int32, (8, CHUNK), 0).astype(jnp.float32)
    wave_rows = row * wave
    length = len_scr[pl.ds(g, 1), :]
    inverse = 1.0 / length
    base = phase(wave_rows, length, inverse)
    outer = phase(wave_rows * float(FINE), length, inverse)
    step = times((base[0][7:8], base[1][7:8]), (base[0][1:2], base[1][1:2]))
    jump = times((outer[0][7:8], outer[1][7:8]), (outer[0][1:2], outer[1][1:2]))
    twice = jnp.broadcast_to(2.0 * step[0], base[0].shape)
    second = times(base, step)
    cos_rows, sin_rows = [base[0], second[0]], [base[1], second[1]]
    for q in range(2, FINE // 8):
        cos_rows.append(twice * cos_rows[-1] - cos_rows[-2])
        sin_rows.append(twice * sin_rows[-1] - sin_rows[-2])
    cos_table = jnp.concatenate(cos_rows, axis=0).astype(jnp.bfloat16)
    sin_table = jnp.concatenate(sin_rows, axis=0).astype(jnp.bfloat16)
    x = x_scr[g]
    real = jnp.dot(x, cos_table, preferred_element_type=jnp.float32)
    imag = jnp.dot(x, sin_table, preferred_element_type=jnp.float32)
    jump = (jnp.broadcast_to(jump[0], row.shape), jnp.broadcast_to(jump[1], row.shape))
    live = (wave >= 1.0) & (wave < float(top_wave)) & (2.0 * wave < length)
    for l in range(levels):
        last = per_circle // 8 - 1
        at = 48 * l + 8 * last
        total = (real[at : at + 8], imag[at : at + 8])
        for q in range(last - 1, -1, -1):
            at = 48 * l + 8 * q
            turned = times(total, jump)
            total = (turned[0] + real[at : at + 8], turned[1] + imag[at : at + 8])
        total = times(total, outer)
        for c in range(2):
            value = jnp.sum(total[c], axis=0, keepdims=True)
            coef_scr[2 * l + c, pl.ds(g, 1), :] = jnp.where(live, value, 0.0)


def pack_tiles(first, coef_scr, send_scr):
    circles = coef_scr.shape[1]
    quarter = lax.broadcasted_iota(jnp.int32, (circles, 128), 1) // 32
    for block in range(CHUNK // 128):
        parts = [coef_scr[k, :, block * 128 : (block + 1) * 128] for k in range(4)]
        for to in range(4):
            value = parts[to]
            for k in range(4):
                if k != to:
                    value = jnp.where(quarter == k, pltpu.roll(parts[k], (32 * (k - to)) % 128, 1), value)
            send_scr[first + block * 4 + to] = value.astype(jnp.bfloat16)


def whole_kernel(
    top_wave, bands, groups, slot_dev,
    grid_ref, below_ref, above_ref, donor_ref, tile_ref, kern_ref, len_ref, wave_ref, lane_wave_ref,
    legendre_ref, out_ref,
    pool_scr, diag_scr, idx_scr, x_scr, len_scr, coef_scr, send_lat, recv_lat, send_lev, recv_lev, leg_scr,
    sems, leg_sem
):
    levels, blocks, lanes = grid_ref.shape
    circles = x_scr.shape[0]
    per_circle = blocks // circles
    band, group = lax.axis_index("lat"), lax.axis_index("lev")
    fetch = pltpu.make_async_copy(legendre_ref, leg_scr, leg_sem)
    fetch.start()
    barrier = pltpu.get_barrier_semaphore()

    def greet_lat(i, carry):
        pl.semaphore_signal(barrier, inc=1, device_id={"lat": lax.rem(band + i, bands)}, device_id_type=MESH)
        return carry

    def greet_lev(i, carry):
        pl.semaphore_signal(barrier, inc=1, device_id={"lev": lax.rem(group + i, groups)}, device_id_type=MESH)
        return carry

    lax.fori_loop(1, bands, greet_lat, 0)
    lax.fori_loop(1, groups, greet_lev, 0)

    fill_donors(grid_ref, below_ref, above_ref, donor_ref, tile_ref, kern_ref, pool_scr, diag_scr, idx_scr)
    interpolate(band, len_ref, pool_scr, diag_scr, idx_scr, x_scr, len_scr)
    pl.semaphore_wait(barrier, bands + groups - 2)

    chunks = wave_ref.shape[0]
    per_chunk = bands // chunks

    def lat_copy(source, to):
        return pltpu.make_async_remote_copy(
            src_ref=send_lat.at[source], dst_ref=recv_lat.at[band], send_sem=sems.at[0], recv_sem=sems.at[1],
            device_id={"lat": to}, device_id_type=MESH,
        )

    def chunk_step(step, carry):
        chunk = lax.rem(step + band // per_chunk, chunks)
        wave = wave_ref[chunk]

        def circle(i, inner):
            for k in range(PAIR):
                transform_circle(i * PAIR + k, wave, top_wave, levels, per_circle, x_scr, len_scr, coef_scr)
            return inner

        lax.fori_loop(0, circles // PAIR, circle, 0)
        pack_tiles(chunk * per_chunk, coef_scr, send_lat)
        for i in range(per_chunk):
            to = chunk * per_chunk + i

            @pl.when(to != band)
            def _():
                lat_copy(to, to).start()

        return carry

    lax.fori_loop(0, chunks, chunk_step, 0)
    recv_lat[band] = send_lat[band]
    some = pl.ds(0, bands - 1)
    bulk = pltpu.make_async_remote_copy(
        src_ref=send_lat.at[some], dst_ref=recv_lat.at[some], send_sem=sems.at[0], recv_sem=sems.at[1],
        device_id={"lat": lax.rem(band + 1, bands)}, device_id_type=MESH,
    )
    bulk.wait()

    target = lax.broadcasted_iota(jnp.int32, (128, 128), 0)
    source = lax.broadcasted_iota(jnp.int32, (128, 128), 1)
    share = 4 * slot_dev
    wanted = (target % share) // slot_dev * (groups * slot_dev) + target // share * slot_dev + target % slot_dev
    pick = jnp.where(source == wanted, 1.0, 0.0).astype(jnp.bfloat16)
    arrived = recv_lat[...].reshape(bands * circles, 128)
    turned = lax.dot_general(pick, arrived, (((1,), (1,)), ((), ())), preferred_element_type=jnp.float32)
    for v in range(groups):
        send_lev[v] = turned[v * share : (v + 1) * share].astype(jnp.bfloat16)

    def send_group(i, carry):
        to = lax.rem(group + i, groups)
        pltpu.make_async_remote_copy(
            src_ref=send_lev.at[to], dst_ref=recv_lev.at[group], send_sem=sems.at[2], recv_sem=sems.at[3],
            device_id={"lev": to}, device_id_type=MESH,
        ).start()
        return carry

    lax.fori_loop(1, groups, send_group, 0)
    recv_lev[group] = send_lev[group]
    some = pl.ds(0, groups - 1)
    bulk = pltpu.make_async_remote_copy(
        src_ref=send_lev.at[some], dst_ref=recv_lev.at[some], send_sem=sems.at[2], recv_sem=sems.at[3],
        device_id={"lev": lax.rem(group + 1, groups)}, device_id_type=MESH,
    )
    bulk.wait()
    fetch.wait()
    left = jnp.concatenate([recv_lev[v].astype(jnp.float32) for v in range(groups)], axis=0).astype(jnp.bfloat16)
    first = (band * groups + group) * slot_dev
    width = 256
    for at in range(0, top_wave, width):
        slot = lax.broadcasted_iota(jnp.int32, (128, width), 0) % slot_dev
        order = lax.broadcasted_iota(jnp.int32, (128, width), 1) + at
        value = jnp.zeros((128, width), jnp.float32)
        for s in range(slot_dev):
            product = jnp.dot(left, leg_scr[s, :, at : at + width], preferred_element_type=jnp.float32)
            value = jnp.where((slot == s) & (order >= lane_wave_ref[first + s]), product, value)
        out_ref[:, at : at + width] = value.astype(jnp.bfloat16)


def transform_all(
    grid, below, above, donor, choice, kernels, lengths, slot_wave, legendre, bands, groups
):
    levels, blocks, lanes = grid.shape
    circles = blocks * lanes // PTS
    slots = slot_wave.shape[0]
    slot_dev, across, top_wave = legendre.shape
    share = 4 * slot_dev
    vmem = pl.BlockSpec(memory_space=pltpu.VMEM)
    smem = pl.BlockSpec(memory_space=pltpu.SMEM)
    waves = slot_wave.astype(jnp.float32).reshape(slots // CHUNK, 1, CHUNK)
    return pl.pallas_call(
        functools.partial(whole_kernel, top_wave, bands, groups, slot_dev),
        out_shape=jax.ShapeDtypeStruct((groups * share, top_wave), jnp.bfloat16),
        in_specs=[vmem] * 6 + [smem, vmem, smem, pl.BlockSpec(memory_space=pl.ANY)],
        out_specs=vmem,
        scratch_shapes=[
            pltpu.VMEM((blocks + 2 * below.shape[1], levels * lanes), jnp.bfloat16),
            pltpu.VMEM((kernels.shape[0], levels * lanes, levels * lanes), jnp.bfloat16),
            pltpu.VMEM((8, blocks), jnp.float32),
            pltpu.VMEM((circles, 96, lanes), jnp.bfloat16),
            pltpu.VMEM((circles, CHUNK), jnp.float32),
            pltpu.VMEM((4, circles, CHUNK), jnp.float32),
            pltpu.VMEM((bands, circles, 128), jnp.bfloat16),
            pltpu.VMEM((bands, circles, 128), jnp.bfloat16),
            pltpu.VMEM((groups, share, across), jnp.bfloat16),
            pltpu.VMEM((groups, share, across), jnp.bfloat16),
            pltpu.VMEM(legendre.shape, jnp.bfloat16),
            pltpu.SemaphoreType.DMA((4,)),
            pltpu.SemaphoreType.DMA,
        ],
        compiler_params=pltpu.CompilerParams(
            vmem_limit_bytes=40 * 1024 * 1024, collective_id=0, has_side_effects=True
        ),
        name="interpolate_transform_exchange",
    )(grid, below, above, donor, choice, kernels, lengths, waves, slot_wave, legendre)


def shift_bands(outgoing, cap):
    size = lax.axis_size("lat")
    up = [(i, i + 1) for i in range(size - 1)]
    down = [(j, i) for i, j in up]
    below = lax.ppermute(outgoing[:, cap:], "lat", up)
    above = lax.ppermute(outgoing[:, :cap], "lat", down)
    return below, above


def body(
    grid_field, send_blocks, donor_index, tile_choice, kernel_tiles, circle_len, slot_wave, legendre
):
    levels, blocks, lanes = grid_field.shape
    cap = send_blocks.shape[2]
    top_wave = legendre.shape[2]
    slot_dev = legendre.shape[0]
    bands = lax.axis_size("lat")
    level_groups = lax.axis_size("lev")
    outgoing = jnp.take(grid_field, send_blocks[0].reshape(-1), axis=1)
    below, above = shift_bands(outgoing, cap)
    spectra = transform_all(
        grid_field, below, above, donor_index.T, tile_choice.T, kernel_tiles, circle_len,
        slot_wave, legendre, bands, level_groups,
    )
    return spectra.reshape(level_groups * levels, 2, slot_dev, top_wave)


def solution(mesh):
    return jax.shard_map(
        body,
        mesh=mesh,
        in_specs=(
            P("lev", "lat", None),
            P("lat", None, None),
            P("lat", None),
            P("lat", None),
            P(),
            P(),
            P(),
            P(("lat", "lev"), None, None),
        ),
        out_specs=P(None, None, ("lat", "lev"), None),
        check_vma=False,
    )
```

time: 105 us -> 75.1 us (0.72)
  starting transfers between devices: 37.2 us -> 6.74 us
  Pallas kernels: 28 us -> 54.3 us
  waiting for transfers between devices: 22.8 us -> 0.59 us
  matrix products: 2.89 us -> 0 us
  local copies, waits for them, and re-layouts: 11.1 us -> 9.91 us
    all_to_all x2 -> x0, starting transfers between devices: 30.5 us -> none  [the longest x1 19.2 us: body(): lax.all_to_all(tiles_out, 'lat', split_axis=0, concat_axis=0, tiled=True)]
    pallas_call x1, Pallas kernels: 28 us -> 54.3 us  [transform_all(): pl.pallas_call(functools.partial(whole_kernel, top_wave, bands, groups, s...]
    all_to_all x2 -> x0, waiting for transfers between devices: 22.2 us -> none  [the longest x1 12.1 us: body(): lax.all_to_all(tiles_out, 'lat', split_axis=0, concat_axis=0, tiled=True)]
    dot_general x1 -> x0, matrix products: 2.89 us -> none  [body(): jnp.einsum('rsg,sgn->rsn', gathered, legendre, preferred_element_type=jnp...]
    unnamed x10 -> x14, local copies, waits for them, and re-layouts: 3.99 us -> 6.79 us
    reshape x4 -> x1, local copies, waits for them, and re-layouts: 2.05 us -> 0.01 us  [transform_all(): waves = slot_wave.astype(jnp.float32).reshape(slots // CHUNK, 1, CHUNK)]
  transfers between devices with their start and end apart: 4 -> 2, of which waited for: 3 -> 1; matrix products, arithmetic and copies ran while one was open for 1% -> 1% of each run, Pallas kernels for 0% -> 0%
where the time goes in v2:
time: 75.1 us; the launch traced here: 73.8 us
  Pallas kernels  54.3 us (72%)
  local copies, waits for them, and re-layouts  9.91 us (13%)
  starting transfers between devices  6.74 us (9%)
  other arithmetic  2.18 us (3%)
    pallas_call x1, Pallas kernels, transform_all(): pl.pallas_call(functools.partial(whole_kernel, top_wave, bands, groups, s...  54.3 us
    unnamed x14, local copies, waits for them, and re-layouts  6.79 us
    ppermute x1, starting transfers between devices, shift_bands(): below = lax.ppermute(outgoing[:, cap:], 'lat', up)  5.45 us
    gather x1, local copies, waits for them, and re-layouts, body(): outgoing = jnp.take(grid_field, send_blocks[0].reshape(-1), axis=1)  2.24 us
  transfers between devices with their start and end apart: 2, of which 1 were waited for; matrix products, arithmetic and copies ran while one was open for 1% of the time, Pallas kernels for 0%

profile of v2, /device:TPU:1, one launch (start us, length us, event | category | flops | bytes accessed | tf_op | source)
XLA Modules:
  0.0 73.8 jit_solution(15697427989410171461)
XLA Ops:
  0.0 0.7 compare_and_fusion
  0.7 0.7 compare_select_fusion
  1.4 2.2 %gather_fusion = bf16[256,2,128]{2,0,1:T(8,128)(2,1)S(1)} fusion(bf16[2,640,128]{2,1,0:T(8,128)(2,1)} %grid_ref.1, s32[1024]{0:T(1024)S(1)} %pad_clamp_fusion), kind=kCustom, calls=%fused_computation | custom fusion | bytes 263168 | tf_op jit(solution)/shard_map/jit(_take)/gather | solution.py:305
  3.6 0.1 select_bitcast_fusion
  3.8 1.3 %collective-permute-start.1 = (bf16[2,128,128]{2,1,0:T(8,128)(2,1)S(1)}, bf16[2,128,128]{2,1,0:T(8,128)(2,1)S(1)}, u32[]{:S(2)}, u32[]{:S(2)}) collective-permute-start(bf16[2,128,128]{2,1,0:T(8,128)(2,1)S(1)} %get-tuple-element.5), channel_id=1, source_target_pairs={{16,0},{32,16},{48,32},{64,48},{80,64},{96,80},{112,96},{128,112},... | collective-permute-start | bytes 196616 | tf_op jit(solution)/shard_map/ppermute | solution.py:292
  5.1 5.4 %collective-permute-start = (bf16[2,128,128]{2,1,0:T(8,128)(2,1)S(1)}, bf16[2,128,128]{2,1,0:T(8,128)(2,1)S(1)}, u32[]{:S(2)}, u32[]{:S(2)}) collective-permute-start(bf16[2,128,128]{2,1,0:T(8,128)(2,1)S(1)} %get-tuple-element.6), channel_id=1, source_target_pairs={{0,16},{16,32},{32,48},{48,64},{64,80},{80,96},{96,112},{112,128},... | collective-permute-start | bytes 196616 | tf_op jit(solution)/shard_map/ppermute | solution.py:291
  10.5 0.7 convert_element_type.3
  11.2 0.0 collective-permute-done.1.above_ref
  11.2 0.6 collective-permute-done.below_ref
  11.8 0.0 copy-start
  11.8 1.0 %copy-done = bf16[2,640,128]{2,1,0:T(8,128)(2,1)S(1)} copy-done((bf16[2,640,128]{2,1,0:T(8,128)(2,1)S(1)}, bf16[2,640,128]{2,1,0:T(8,128)(2,1)}, u32[]{:S(2)}) %copy-start) | copy-done | bytes 327704
  12.8 0.0 copy-start.1
  12.8 2.1 %copy-done.1 = bf16[2,768,1280]{2,1,0:T(8,128)(2,1)S(1)} copy-done((bf16[2,768,1280]{2,1,0:T(8,128)(2,1)S(1)}, bf16[2,768,1280]{2,1,0:T(8,128)(2,1)}, u32[]{:S(2)}) %copy-start.1) | copy-done | bytes 3932184
  14.9 0.0 copy-start.2
  14.9 0.9 %copy-done.2 = bf16[8,128,128]{2,1,0:T(8,128)(2,1)S(1)} copy-done((bf16[8,128,128]{2,1,0:T(8,128)(2,1)S(1)}, bf16[8,128,128]{2,1,0:T(8,128)(2,1)}, u32[]{:S(2)}) %copy-start.2) | copy-done | bytes 262168
  15.9 0.0 copy-start.3
  15.9 0.7 copy-done.3
  16.6 0.0 copy-start.4
  16.6 0.7 copy-done.4
  17.2 0.0 copy-start.5
  17.2 0.7 copy-done.5
  17.9 0.0 copy-start.6
  17.9 0.7 copy-done.6
  18.6 54.3 %interpolate_transform_exchange.1 = bf16[128,1280]{1,0:T(8,128)(2,1)S(1)} custom-call(bf16[2,640,128]{2,1,0:T(8,128)(2,1)S(1)} %copy-done, bf16[2,128,128]{2,1,0:T(8,128)(2,1)S(1)} %collective-permute-done.below_ref, bf16[2,128,128]{2,1,0:T(8,128)(2,1)S(1)} %collective-permute-done.1.above_ref, s32[2,640]{1,0:T(2,128)S(1)} %bitcast.8, s32[2,640]{1,0:T(2,128)S(1)} %bitcast.9, ...), custom_call_target="tpu_custom_call" | custom-call | tf_op jit(solution)/shard_map/interpolate_transform_exchange/pallas_call | solution.py:260
  72.9 0.8 %reshape.41 = bf16[32,2,2,1280]{3,2,1,0:T(2,128)(2,1)} reshape(bf16[128,1280]{1,0:T(8,128)(2,1)S(1)} %interpolate_transform_exchange.1) | data formatting | bytes 655360 | tf_op jit(solution)/shard_map/reshape | solution.py:311
  (3 shorter events, 0.0 us)
Async XLA Ops:
  3.8 7.5 %collective-permute-start.1 = (bf16[2,128,128]{2,1,0:T(8,128)(2,1)S(1)}, bf16[2,128,128]{2,1,0:T(8,128)(2,1)S(1)}, u32[]{:S(2)}, u32[]{:S(2)}) collective-permute-start(bf16[2,128,128]{2,1,0:T(8,128)(2,1)S(1)} %get-tuple-element.5), channel_id=1, source_target_pairs={{16,0},{32,16},{48,32},{64,48},{80,64},{96,80},{112,96},{128,112},... | collective-permute-start | bytes 196616 | tf_op jit(solution)/shard_map/ppermute | solution.py:292
  5.1 6.8 %collective-permute-start = (bf16[2,128,128]{2,1,0:T(8,128)(2,1)S(1)}, bf16[2,128,128]{2,1,0:T(8,128)(2,1)S(1)}, u32[]{:S(2)}, u32[]{:S(2)}) collective-permute-start(bf16[2,128,128]{2,1,0:T(8,128)(2,1)S(1)} %get-tuple-element.6), channel_id=1, source_target_pairs={{0,16},{16,32},{32,48},{48,64},{64,80},{80,96},{96,112},{112,128},... | collective-permute-start | bytes 196616 | tf_op jit(solution)/shard_map/ppermute | solution.py:291
  11.8 1.0 %copy-start = (bf16[2,640,128]{2,1,0:T(8,128)(2,1)S(1)}, bf16[2,640,128]{2,1,0:T(8,128)(2,1)}, u32[]{:S(2)}) copy-start(bf16[2,640,128]{2,1,0:T(8,128)(2,1)} %grid_ref.1) | copy-start | bytes 983044
  12.8 2.1 %copy-start.1 = (bf16[2,768,1280]{2,1,0:T(8,128)(2,1)S(1)}, bf16[2,768,1280]{2,1,0:T(8,128)(2,1)}, u32[]{:S(2)}) copy-start(bf16[2,768,1280]{2,1,0:T(8,128)(2,1)} %legendre_ref.1) | copy-start | bytes 11796484
  14.9 0.9 %copy-start.2 = (bf16[8,128,128]{2,1,0:T(8,128)(2,1)S(1)}, bf16[8,128,128]{2,1,0:T(8,128)(2,1)}, u32[]{:S(2)}) copy-start(bf16[8,128,128]{2,1,0:T(8,128)(2,1)} %kern_ref.1) | copy-start | bytes 786436
  15.9 0.7 copy-start.3
  16.6 0.7 copy-start.4
  17.2 0.7 copy-start.5
  17.9 0.7 copy-start.6

commit v3 on v2

--- a/solution.py
+++ b/solution.py
@@ -10,7 +10,8 @@
 PTS = 5120
 FINE = 128
 CHUNK = 256
-PAIR = 2
+PAIR = 8
+EARLY = 4
 
 SIN_COEF = (3.1415927410125732, -5.167709827423096, 2.550076961517334, -0.5982874631881714, 0.07764891535043716)
 COS_COEF = (1.0, -4.934792518615723, 4.058409690856934, -1.331863284111023, 0.21965928375720978)
@@ -39,31 +40,12 @@
 MESH = pl.DeviceIdType.MESH
 
 
-def fill_donors(grid_ref, below_ref, above_ref, donor_ref, tile_ref, kern_ref, pool_scr, diag_scr, idx_scr):
-    levels, blocks, lanes = grid_ref.shape
-    cap = below_ref.shape[1]
-    for l in range(levels):
-        cols = slice(l * lanes, (l + 1) * lanes)
-        pool_scr[0:blocks, cols] = grid_ref[l]
-        pool_scr[blocks : blocks + cap, cols] = below_ref[l]
-        pool_scr[blocks + cap : blocks + 2 * cap, cols] = above_ref[l]
-    diag_scr[...] = jnp.zeros_like(diag_scr)
-    for t in range(kern_ref.shape[0]):
-        for l in range(levels):
-            cols = slice(l * lanes, (l + 1) * lanes)
-            diag_scr[t, cols, cols] = kern_ref[t]
-    idx_scr[...] = jnp.zeros_like(idx_scr)
-    idx_scr[0:2, :] = donor_ref[...].astype(jnp.float32)
-    idx_scr[2:4, :] = tile_ref[...].astype(jnp.float32)
-
-
-def interpolate(band, len_ref, pool_scr, diag_scr, idx_scr, x_scr, len_scr):
+def interpolate(band, len_ref, columns, pool_scr, diag_scr, x_scr):
     pool_size, width = pool_scr.shape
     tiles = diag_scr.shape[0]
     circles, _, lanes = x_scr.shape
     levels = width // lanes
-    per_circle = idx_scr.shape[1] // circles
-    columns = idx_scr[...].T
+    per_circle = columns.shape[0] // circles
     group = 4
     rows = group * per_circle
     for start in range(0, circles, group):
@@ -86,30 +68,36 @@
                 piece = squared[c * per_circle : (c + 1) * per_circle, l * lanes : (l + 1) * lanes]
                 piece = jnp.where(spot < n, piece, 0.0).astype(jnp.bfloat16)
                 x_scr[start + c, 48 * l : 48 * l + per_circle, :] = piece
-            len_scr[start + c : start + c + 1, :] = jnp.full((1, CHUNK), n, jnp.int32).astype(jnp.float32)
-
-
-def transform_circle(g, wave, top_wave, levels, per_circle, x_scr, len_scr, coef_scr):
+
+
+def circle_tables(g, chunk, wave, len_scr, table_scr, outer_scr):
     row = lax.broadcasted_iota(jnp.int32, (8, CHUNK), 0).astype(jnp.float32)
     wave_rows = row * wave
     length = len_scr[pl.ds(g, 1), :]
     inverse = 1.0 / length
     base = phase(wave_rows, length, inverse)
     outer = phase(wave_rows * float(FINE), length, inverse)
+    outer_scr[chunk, g, 0:8, :] = outer[0]
+    outer_scr[chunk, g, 8:16, :] = outer[1]
     step = times((base[0][7:8], base[1][7:8]), (base[0][1:2], base[1][1:2]))
-    jump = times((outer[0][7:8], outer[1][7:8]), (outer[0][1:2], outer[1][1:2]))
     twice = jnp.broadcast_to(2.0 * step[0], base[0].shape)
     second = times(base, step)
-    cos_rows, sin_rows = [base[0], second[0]], [base[1], second[1]]
-    for q in range(2, FINE // 8):
-        cos_rows.append(twice * cos_rows[-1] - cos_rows[-2])
-        sin_rows.append(twice * sin_rows[-1] - sin_rows[-2])
-    cos_table = jnp.concatenate(cos_rows, axis=0).astype(jnp.bfloat16)
-    sin_table = jnp.concatenate(sin_rows, axis=0).astype(jnp.bfloat16)
+    for part in range(2):
+        rows = [base[part], second[part]]
+        for q in range(2, FINE // 8):
+            rows.append(twice * rows[-1] - rows[-2])
+        table = jnp.concatenate(rows, axis=0).astype(jnp.bfloat16)
+        table_scr[chunk, g, :, part * CHUNK : (part + 1) * CHUNK] = table
+
+
+def transform_circle(g, chunk, wave, top_wave, levels, per_circle, x_scr, len_scr, table_scr, outer_scr, coef_scr):
+    length = len_scr[pl.ds(g, 1), :]
+    outer = (outer_scr[chunk, g, 0:8, :], outer_scr[chunk, g, 8:16, :])
+    jump = times((outer[0][7:8], outer[1][7:8]), (outer[0][1:2], outer[1][1:2]))
+    jump = (jnp.broadcast_to(jump[0], (8, CHUNK)), jnp.broadcast_to(jump[1], (8, CHUNK)))
     x = x_scr[g]
-    real = jnp.dot(x, cos_table, preferred_element_type=jnp.float32)
-    imag = jnp.dot(x, sin_table, preferred_element_type=jnp.float32)
-    jump = (jnp.broadcast_to(jump[0], row.shape), jnp.broadcast_to(jump[1], row.shape))
+    real = jnp.dot(x, table_scr[chunk, g, :, :CHUNK], preferred_element_type=jnp.float32)
+    imag = jnp.dot(x, table_scr[chunk, g, :, CHUNK:], preferred_element_type=jnp.float32)
     live = (wave >= 1.0) & (wave < float(top_wave)) & (2.0 * wave < length)
     for l in range(levels):
         last = per_circle // 8 - 1
@@ -140,15 +128,27 @@
 
 def whole_kernel(
     top_wave, bands, groups, slot_dev,
-    grid_ref, below_ref, above_ref, donor_ref, tile_ref, kern_ref, len_ref, wave_ref, lane_wave_ref,
-    legendre_ref, out_ref,
-    pool_scr, diag_scr, idx_scr, x_scr, len_scr, coef_scr, send_lat, recv_lat, send_lev, recv_lev, leg_scr,
-    sems, leg_sem
+    grid_ref, send_ref, donor_ref, tile_ref, kern_ref, len_hbm, wave_hbm, wave_rows_ref, legendre_ref, out_ref,
+    pool_scr, diag_scr, send_scr, donor_scr, tile_scr, idx_scr, halo_scr, len_ref, slot_ref, wave_scr, waves_scr,
+    x_scr, len_scr, table_scr, outer_scr, coef_scr, send_lat, recv_lat, send_lev, recv_lev, leg_scr,
+    sems, halo_sems, load_sems, leg_sem
 ):
     levels, blocks, lanes = grid_ref.shape
+    cap = halo_scr.shape[1]
     circles = x_scr.shape[0]
     per_circle = blocks // circles
     band, group = lax.axis_index("lat"), lax.axis_index("lev")
+    pairs = [(len_hbm, len_ref), (wave_rows_ref, wave_scr), (send_ref, send_scr), (donor_ref, donor_scr), (tile_ref, tile_scr)]
+    for l in range(levels):
+        cols = slice(l * lanes, (l + 1) * lanes)
+        pairs.append((grid_ref.at[l], pool_scr.at[0:blocks, cols]))
+    for l in range(levels):
+        cols = slice(l * lanes, (l + 1) * lanes)
+        pairs.append((kern_ref, diag_scr.at[:, cols, cols]))
+    pairs.append((wave_hbm, slot_ref))
+    loads = [pltpu.make_async_copy(src, dst, load_sems.at[i]) for i, (src, dst) in enumerate(pairs)]
+    for load in loads:
+        load.start()
     fetch = pltpu.make_async_copy(legendre_ref, leg_scr, leg_sem)
     fetch.start()
     barrier = pltpu.get_barrier_semaphore()
@@ -164,11 +164,87 @@
     lax.fori_loop(1, bands, greet_lat, 0)
     lax.fori_loop(1, groups, greet_lev, 0)
 
-    fill_donors(grid_ref, below_ref, above_ref, donor_ref, tile_ref, kern_ref, pool_scr, diag_scr, idx_scr)
-    interpolate(band, len_ref, pool_scr, diag_scr, idx_scr, x_scr, len_scr)
+    for l in range(levels):
+        for m in range(levels):
+            if l != m:
+                rows, cols = slice(l * lanes, (l + 1) * lanes), slice(m * lanes, (m + 1) * lanes)
+                diag_scr[:, rows, cols] = jnp.zeros((diag_scr.shape[0], lanes, lanes), jnp.bfloat16)
+    idx_scr[...] = jnp.zeros_like(idx_scr)
+
+    @pl.when(band == 0)
+    def _():
+        pool_scr[blocks : blocks + cap, :] = jnp.zeros((cap, levels * lanes), jnp.bfloat16)
+
+    @pl.when(band == bands - 1)
+    def _():
+        pool_scr[blocks + cap : blocks + 2 * cap, :] = jnp.zeros((cap, levels * lanes), jnp.bfloat16)
+
+    loads[0].wait()
+    loads[1].wait()
+    for g in range(circles):
+        n = len_ref[band * circles + g]
+        len_scr[g : g + 1, :] = jnp.full((1, CHUNK), n, jnp.int32).astype(jnp.float32)
+    chunks = waves_scr.shape[0]
+    each = CHUNK // 128
+    for chunk in range(chunks):
+        for k in range(each):
+            at = chunk * each + k
+            waves_scr[chunk, :, k * 128 : (k + 1) * 128] = wave_scr[at : at + 1, :].astype(jnp.float32)
+
+    def table_step(step, carry):
+        wave = waves_scr[step // (circles // PAIR)]
+        for k in range(PAIR):
+            g = step % (circles // PAIR) * PAIR + k
+            circle_tables(g, step // (circles // PAIR), wave, len_scr, table_scr, outer_scr)
+        return carry
+
+    ahead = chunks * EARLY // 6 * (circles // PAIR)
+    lax.fori_loop(0, ahead, table_step, 0)
+
+    for load in loads[2:]:
+        load.wait()
+    idx_scr[0:2, :] = donor_scr[...].astype(jnp.float32)
+    idx_scr[2:4, :] = tile_scr[...].astype(jnp.float32)
+    idx_scr[4:6, 0:cap] = send_scr[0].astype(jnp.float32)
+    columns = idx_scr[...].T
+    own = lax.broadcasted_iota(jnp.int32, (cap, blocks), 1).astype(jnp.float32)
+    for side in range(2):
+        hot = jnp.where(own == columns[0:cap, 4 + side : 5 + side], 1.0, 0.0).astype(jnp.bfloat16)
+        rows = jnp.dot(hot, pool_scr[0:blocks, :], preferred_element_type=jnp.float32)
+        halo_scr[side] = rows.astype(jnp.bfloat16)
     pl.semaphore_wait(barrier, bands + groups - 2)
 
-    chunks = wave_ref.shape[0]
+    down = pltpu.make_async_remote_copy(
+        src_ref=halo_scr.at[0], dst_ref=pool_scr.at[blocks + cap : blocks + 2 * cap], send_sem=halo_sems.at[0],
+        recv_sem=halo_sems.at[1], device_id={"lat": lax.rem(band + bands - 1, bands)}, device_id_type=MESH,
+    )
+    up = pltpu.make_async_remote_copy(
+        src_ref=halo_scr.at[1], dst_ref=pool_scr.at[blocks : blocks + cap], send_sem=halo_sems.at[2],
+        recv_sem=halo_sems.at[3], device_id={"lat": lax.rem(band + 1, bands)}, device_id_type=MESH,
+    )
+
+    @pl.when(band > 0)
+    def _():
+        down.start()
+
+    @pl.when(band < bands - 1)
+    def _():
+        up.start()
+
+    lax.fori_loop(ahead, chunks * (circles // PAIR), table_step, 0)
+
+    @pl.when(band > 0)
+    def _():
+        down.wait_send()
+        up.wait_recv()
+
+    @pl.when(band < bands - 1)
+    def _():
+        up.wait_send()
+        down.wait_recv()
+
+    interpolate(band, len_ref, columns, pool_scr, diag_scr, x_scr)
+
     per_chunk = bands // chunks
 
     def lat_copy(source, to):
@@ -179,11 +255,13 @@
 
     def chunk_step(step, carry):
         chunk = lax.rem(step + band // per_chunk, chunks)
-        wave = wave_ref[chunk]
+        wave = waves_scr[chunk]
 
         def circle(i, inner):
             for k in range(PAIR):
-                transform_circle(i * PAIR + k, wave, top_wave, levels, per_circle, x_scr, len_scr, coef_scr)
+                transform_circle(
+                    i * PAIR + k, chunk, wave, top_wave, levels, per_circle, x_scr, len_scr, table_scr, outer_scr, coef_scr
+                )
             return inner
 
         lax.fori_loop(0, circles // PAIR, circle, 0)
@@ -242,55 +320,8 @@
         value = jnp.zeros((128, width), jnp.float32)
         for s in range(slot_dev):
             product = jnp.dot(left, leg_scr[s, :, at : at + width], preferred_element_type=jnp.float32)
-            value = jnp.where((slot == s) & (order >= lane_wave_ref[first + s]), product, value)
+            value = jnp.where((slot == s) & (order >= slot_ref[first + s]), product, value)
         out_ref[:, at : at + width] = value.astype(jnp.bfloat16)
-
-
-def transform_all(
-    grid, below, above, donor, choice, kernels, lengths, slot_wave, legendre, bands, groups
-):
-    levels, blocks, lanes = grid.shape
-    circles = blocks * lanes // PTS
-    slots = slot_wave.shape[0]
-    slot_dev, across, top_wave = legendre.shape
-    share = 4 * slot_dev
-    vmem = pl.BlockSpec(memory_space=pltpu.VMEM)
-    smem = pl.BlockSpec(memory_space=pltpu.SMEM)
-    waves = slot_wave.astype(jnp.float32).reshape(slots // CHUNK, 1, CHUNK)
-    return pl.pallas_call(
-        functools.partial(whole_kernel, top_wave, bands, groups, slot_dev),
-        out_shape=jax.ShapeDtypeStruct((groups * share, top_wave), jnp.bfloat16),
-        in_specs=[vmem] * 6 + [smem, vmem, smem, pl.BlockSpec(memory_space=pl.ANY)],
-        out_specs=vmem,
-        scratch_shapes=[
-            pltpu.VMEM((blocks + 2 * below.shape[1], levels * lanes), jnp.bfloat16),
-            pltpu.VMEM((kernels.shape[0], levels * lanes, levels * lanes), jnp.bfloat16),
-            pltpu.VMEM((8, blocks), jnp.float32),
-            pltpu.VMEM((circles, 96, lanes), jnp.bfloat16),
-            pltpu.VMEM((circles, CHUNK), jnp.float32),
-            pltpu.VMEM((4, circles, CHUNK), jnp.float32),
-            pltpu.VMEM((bands, circles, 128), jnp.bfloat16),
-            pltpu.VMEM((bands, circles, 128), jnp.bfloat16),
-            pltpu.VMEM((groups, share, across), jnp.bfloat16),
-            pltpu.VMEM((groups, share, across), jnp.bfloat16),
-            pltpu.VMEM(legendre.shape, jnp.bfloat16),
-            pltpu.SemaphoreType.DMA((4,)),
-            pltpu.SemaphoreType.DMA,
-        ],
-        compiler_params=pltpu.CompilerParams(
-            vmem_limit_bytes=40 * 1024 * 1024, collective_id=0, has_side_effects=True
-        ),
-        name="interpolate_transform_exchange",
-    )(grid, below, above, donor, choice, kernels, lengths, waves, slot_wave, legendre)
-
-
-def shift_bands(outgoing, cap):
-    size = lax.axis_size("lat")
-    up = [(i, i + 1) for i in range(size - 1)]
-    down = [(j, i) for i, j in up]
-    below = lax.ppermute(outgoing[:, cap:], "lat", up)
-    above = lax.ppermute(outgoing[:, :cap], "lat", down)
-    return below, above
 
 
 def body(
@@ -298,17 +329,58 @@
 ):
     levels, blocks, lanes = grid_field.shape
     cap = send_blocks.shape[2]
-    top_wave = legendre.shape[2]
-    slot_dev = legendre.shape[0]
     bands = lax.axis_size("lat")
-    level_groups = lax.axis_size("lev")
-    outgoing = jnp.take(grid_field, send_blocks[0].reshape(-1), axis=1)
-    below, above = shift_bands(outgoing, cap)
-    spectra = transform_all(
-        grid_field, below, above, donor_index.T, tile_choice.T, kernel_tiles, circle_len,
-        slot_wave, legendre, bands, level_groups,
-    )
-    return spectra.reshape(level_groups * levels, 2, slot_dev, top_wave)
+    groups = lax.axis_size("lev")
+    circles = blocks * lanes // PTS
+    slots = slot_wave.shape[0]
+    slot_dev, across, top_wave = legendre.shape
+    share = 2 * levels * slot_dev
+    tiles = kernel_tiles.shape[0]
+    width = levels * lanes
+    chunks = slots // CHUNK
+    bf16, f32, i32 = jnp.bfloat16, jnp.float32, jnp.int32
+    hbm = pl.BlockSpec(memory_space=pltpu.HBM)
+    spectra = pl.pallas_call(
+        functools.partial(whole_kernel, top_wave, bands, groups, slot_dev),
+        out_shape=jax.ShapeDtypeStruct((groups * share, top_wave), bf16),
+        in_specs=[hbm] * 9,
+        out_specs=pl.BlockSpec(memory_space=pltpu.VMEM),
+        scratch_shapes=[
+            pltpu.VMEM((blocks + 2 * cap, width), bf16),
+            pltpu.VMEM((tiles, width, width), bf16),
+            pltpu.VMEM((1, 2, cap), i32),
+            pltpu.VMEM((2, blocks), i32),
+            pltpu.VMEM((2, blocks), i32),
+            pltpu.VMEM((8, blocks), f32),
+            pltpu.VMEM((2, cap, width), bf16),
+            pltpu.SMEM(circle_len.shape, i32),
+            pltpu.SMEM(slot_wave.shape, i32),
+            pltpu.VMEM((slots // 128, 128), i32),
+            pltpu.VMEM((chunks, 1, CHUNK), f32),
+            pltpu.VMEM((circles, 96, lanes), bf16),
+            pltpu.VMEM((circles, CHUNK), f32),
+            pltpu.VMEM((chunks, circles, FINE, 2 * CHUNK), bf16),
+            pltpu.VMEM((chunks, circles, 16, CHUNK), f32),
+            pltpu.VMEM((2 * levels, circles, CHUNK), f32),
+            pltpu.VMEM((bands, circles, 128), bf16),
+            pltpu.VMEM((bands, circles, 128), bf16),
+            pltpu.VMEM((groups, share, across), bf16),
+            pltpu.VMEM((groups, share, across), bf16),
+            pltpu.VMEM(legendre.shape, bf16),
+            pltpu.SemaphoreType.DMA((4,)),
+            pltpu.SemaphoreType.DMA((4,)),
+            pltpu.SemaphoreType.DMA((10,)),
+            pltpu.SemaphoreType.DMA,
+        ],
+        compiler_params=pltpu.CompilerParams(
+            vmem_limit_bytes=56 * 1024 * 1024, collective_id=0, has_side_effects=True
+        ),
+        name="interpolate_transform_exchange",
+    )(
+        grid_field, send_blocks, donor_index.T, tile_choice.T, kernel_tiles, circle_len, slot_wave,
+        slot_wave.reshape(slots // 128, 128), legendre,
+    )
+    return spectra.reshape(groups * levels, 2, slot_dev, top_wave)
 
 
 def solution(mesh):

time: 75.1 us -> 50.4 us (0.67); the launches traced: 73.8 us -> 50.2 us
  local copies, waits for them, and re-layouts: 9.91 us -> 1.82 us
  starting transfers between devices: 6.74 us -> 0 us
  Pallas kernels: 54.3 us -> 48.4 us
  other arithmetic: 2.18 us -> 0 us
    unnamed x14 -> x0, local copies, waits for them, and re-layouts: 6.79 us -> none
    ppermute x2 -> x0, starting transfers between devices: 6.74 us -> none  [the longest x1 5.45 us: shift_bands(): below = lax.ppermute(outgoing[:, cap:], 'lat', up)]
    pallas_call x1, Pallas kernels: 54.3 us -> 48.4 us  [body(): pl.pallas_call(functools.partial(whole_kernel, top_wave, bands, groups, s...]
    gather x1 -> x0, local copies, waits for them, and re-layouts: 2.24 us -> none  [body(): outgoing = jnp.take(grid_field, send_blocks[0].reshape(-1), axis=1)]
    reshape x2 -> x1, local copies, waits for them, and re-layouts: 0.86 us -> 1.82 us  [body(): return spectra.reshape(groups * levels, 2, slot_dev, top_wave)]
    select_n x2 -> x0, other arithmetic: 0.78 us -> none  [body(): outgoing = jnp.take(grid_field, send_blocks[0].reshape(-1), axis=1)]
  transfers between devices with their start and end apart: 2 -> 0, of which waited for: 1 -> 0; matrix products, arithmetic and copies ran while one was open for 1% -> 0% of each run, Pallas kernels for 0% -> 0%
where the time goes in v3:
time: 50.4 us; the launch traced here: 50.2 us
  Pallas kernels  48.4 us (96%)
  local copies, waits for them, and re-layouts  1.82 us (4%)
    pallas_call x1, Pallas kernels, body(): pl.pallas_call(functools.partial(whole_kernel, top_wave, bands, groups, s...  48.4 us
    reshape x1, local copies, waits for them, and re-layouts, body(): return spectra.reshape(groups * levels, 2, slot_dev, top_wave)  1.82 us

profile of v3, /device:TPU:1, one launch (start us, length us, event | category | flops | bytes accessed | tf_op | source)
XLA Modules:
  0.0 50.2 jit_solution(15078778699725886565)
XLA Ops:
  0.0 48.4 %interpolate_transform_exchange.1 = bf16[128,1280]{1,0:T(8,128)(2,1)} custom-call(bf16[2,640,128]{2,1,0:T(8,128)(2,1)} %grid_ref.1, s32[1,2,128]{2,1,0:T(2,128)} %send_ref.1, s32[2,640]{1,0:T(2,128)} %bitcast.4, s32[2,640]{1,0:T(2,128)} %bitcast.5, bf16[8,128,128]{2,1,0:T(8,128)(2,1)} %kern_ref.1, s32[768]{0:T(1024)} %len_hbm.1, s32[1536]{0:T(1024)} %wave_hbm.1, ...), custom_call_target="tpu_custom_call" | custom-call | tf_op jit(solution)/shard_map/interpolate_transform_exchange/pallas_call | solution.py:343
  48.4 1.8 %reshape.7 = bf16[32,2,2,1280]{3,2,1,0:T(2,128)(2,1)} reshape(bf16[128,1280]{1,0:T(8,128)(2,1)} %interpolate_transform_exchange.1) | data formatting | bytes 655360 | tf_op jit(solution)/shard_map/reshape | solution.py:383

commit v4 on v3

--- a/solution.py
+++ b/solution.py
@@ -131,7 +131,7 @@
     grid_ref, send_ref, donor_ref, tile_ref, kern_ref, len_hbm, wave_hbm, wave_rows_ref, legendre_ref, out_ref,
     pool_scr, diag_scr, send_scr, donor_scr, tile_scr, idx_scr, halo_scr, len_ref, slot_ref, wave_scr, waves_scr,
     x_scr, len_scr, table_scr, outer_scr, coef_scr, send_lat, recv_lat, send_lev, recv_lev, leg_scr,
-    sems, halo_sems, load_sems, leg_sem
+    total_scr, sems, lat_sems, lev_sems, halo_sems, load_sems, leg_sems
 ):
     levels, blocks, lanes = grid_ref.shape
     cap = halo_scr.shape[1]
@@ -149,8 +149,13 @@
     loads = [pltpu.make_async_copy(src, dst, load_sems.at[i]) for i, (src, dst) in enumerate(pairs)]
     for load in loads:
         load.start()
-    fetch = pltpu.make_async_copy(legendre_ref, leg_scr, leg_sem)
-    fetch.start()
+    fetches = []
+    for p in range(leg_scr.shape[0]):
+        for k in range(slot_dev):
+            rows = slice(p * leg_scr.shape[2], (p + 1) * leg_scr.shape[2])
+            fetches.append(pltpu.make_async_copy(legendre_ref.at[k, rows], leg_scr.at[p, k], leg_sems.at[p, k]))
+    for fetch in fetches:
+        fetch.start()
     barrier = pltpu.get_barrier_semaphore()
 
     def greet_lat(i, carry):
@@ -246,15 +251,10 @@
     interpolate(band, len_ref, columns, pool_scr, diag_scr, x_scr)
 
     per_chunk = bands // chunks
-
-    def lat_copy(source, to):
-        return pltpu.make_async_remote_copy(
-            src_ref=send_lat.at[source], dst_ref=recv_lat.at[band], send_sem=sems.at[0], recv_sem=sems.at[1],
-            device_id={"lat": to}, device_id_type=MESH,
-        )
+    home = band // per_chunk
 
     def chunk_step(step, carry):
-        chunk = lax.rem(step + band // per_chunk, chunks)
+        chunk = lax.rem(step + home, chunks)
         wave = waves_scr[chunk]
 
         def circle(i, inner):
@@ -271,57 +271,85 @@
 
             @pl.when(to != band)
             def _():
-                lat_copy(to, to).start()
+                pltpu.make_async_remote_copy(
+                    src_ref=send_lat.at[to], dst_ref=recv_lat.at[band], send_sem=sems.at[0],
+                    recv_sem=lat_sems.at[home], device_id={"lat": to}, device_id_type=MESH,
+                ).start()
 
         return carry
 
     lax.fori_loop(0, chunks, chunk_step, 0)
     recv_lat[band] = send_lat[band]
-    some = pl.ds(0, bands - 1)
-    bulk = pltpu.make_async_remote_copy(
-        src_ref=send_lat.at[some], dst_ref=recv_lat.at[some], send_sem=sems.at[0], recv_sem=sems.at[1],
-        device_id={"lat": lax.rem(band + 1, bands)}, device_id_type=MESH,
-    )
-    bulk.wait()
+    next_band = {"lat": lax.rem(band + 1, bands)}
+    next_group = {"lev": lax.rem(group + 1, groups)}
+
+    def lat_wait(start, count, sem):
+        some = pl.ds(start, count)
+        return pltpu.make_async_remote_copy(
+            src_ref=send_lat.at[some], dst_ref=recv_lat.at[some], send_sem=sems.at[0], recv_sem=sem,
+            device_id=next_band, device_id_type=MESH,
+        )
+
+    def lev_wait(src, dst, sem):
+        return pltpu.make_async_remote_copy(
+            src_ref=src, dst_ref=dst, send_sem=sems.at[1], recv_sem=sem, device_id=next_group, device_id_type=MESH,
+        )
 
     target = lax.broadcasted_iota(jnp.int32, (128, 128), 0)
     source = lax.broadcasted_iota(jnp.int32, (128, 128), 1)
     share = 4 * slot_dev
     wanted = (target % share) // slot_dev * (groups * slot_dev) + target // share * slot_dev + target % slot_dev
     pick = jnp.where(source == wanted, 1.0, 0.0).astype(jnp.bfloat16)
-    arrived = recv_lat[...].reshape(bands * circles, 128)
-    turned = lax.dot_general(pick, arrived, (((1,), (1,)), ((), ())), preferred_element_type=jnp.float32)
-    for v in range(groups):
-        send_lev[v] = turned[v * share : (v + 1) * share].astype(jnp.bfloat16)
-
-    def send_group(i, carry):
-        to = lax.rem(group + i, groups)
-        pltpu.make_async_remote_copy(
-            src_ref=send_lev.at[to], dst_ref=recv_lev.at[group], send_sem=sems.at[2], recv_sem=sems.at[3],
-            device_id={"lev": to}, device_id_type=MESH,
-        ).start()
-        return carry
-
-    lax.fori_loop(1, groups, send_group, 0)
-    recv_lev[group] = send_lev[group]
-    some = pl.ds(0, groups - 1)
-    bulk = pltpu.make_async_remote_copy(
-        src_ref=send_lev.at[some], dst_ref=recv_lev.at[some], send_sem=sems.at[2], recv_sem=sems.at[3],
-        device_id={"lev": lax.rem(group + 1, groups)}, device_id_type=MESH,
-    )
-    bulk.wait()
-    fetch.wait()
-    left = jnp.concatenate([recv_lev[v].astype(jnp.float32) for v in range(groups)], axis=0).astype(jnp.bfloat16)
+    span = per_chunk * circles
+    for p in range(chunks):
+        part = lax.rem(home + chunks - p, chunks)
+        lat_wait(part * per_chunk, per_chunk - (p == 0), lat_sems.at[part]).wait_recv()
+        arrived = recv_lat[pl.ds(part * per_chunk, per_chunk)].reshape(span, 128)
+        turned = lax.dot_general(pick, arrived, (((1,), (1,)), ((), ())), preferred_element_type=jnp.float32)
+        for v in range(groups):
+            send_lev[p, v] = turned[v * share : (v + 1) * share].astype(jnp.bfloat16)
+
+        def send_group(i, carry):
+            to = lax.rem(group + i, groups)
+            pltpu.make_async_remote_copy(
+                src_ref=send_lev.at[p, to], dst_ref=recv_lev.at[p, group], send_sem=sems.at[1],
+                recv_sem=lev_sems.at[p], device_id={"lev": to}, device_id_type=MESH,
+            ).start()
+            return carry
+
+        lax.fori_loop(1, groups, send_group, 0)
+        recv_lev[p, group] = send_lev[p, group]
+
+    for fetch in fetches:
+        fetch.wait()
     first = (band * groups + group) * slot_dev
     width = 256
-    for at in range(0, top_wave, width):
-        slot = lax.broadcasted_iota(jnp.int32, (128, width), 0) % slot_dev
-        order = lax.broadcasted_iota(jnp.int32, (128, width), 1) + at
-        value = jnp.zeros((128, width), jnp.float32)
-        for s in range(slot_dev):
-            product = jnp.dot(left, leg_scr[s, :, at : at + width], preferred_element_type=jnp.float32)
-            value = jnp.where((slot == s) & (order >= slot_ref[first + s]), product, value)
-        out_ref[:, at : at + width] = value.astype(jnp.bfloat16)
+    kinds = lax.broadcasted_iota(jnp.int32, (128, span), 0) % slot_dev
+    for p in range(chunks):
+        part = lax.rem(home + chunks - p, chunks)
+        some = pl.ds(0, groups - 1)
+        lev_wait(send_lev.at[p, some], recv_lev.at[p, some], lev_sems.at[p]).wait_recv()
+        left = jnp.concatenate([recv_lev[p, v].astype(jnp.float32) for v in range(groups)], axis=0)
+        left = jnp.concatenate([jnp.where(kinds == s, left, 0.0) for s in range(slot_dev)], axis=1).astype(jnp.bfloat16)
+        for at in range(0, top_wave, width):
+            cols = slice(at, at + width)
+            right = leg_scr[part, :, :, cols].reshape(slot_dev * span, width)
+            value = jnp.dot(left, right, preferred_element_type=jnp.float32)
+            if p > 0:
+                value = value + total_scr[:, cols]
+            if p < chunks - 1:
+                total_scr[:, cols] = value
+                continue
+            slot = lax.broadcasted_iota(jnp.int32, (128, width), 0) % slot_dev
+            order = lax.broadcasted_iota(jnp.int32, (128, width), 1) + at
+            least = jnp.zeros((128, width), jnp.int32)
+            for s in range(slot_dev):
+                least = jnp.where(slot == s, slot_ref[first + s], least)
+            out_ref[:, cols] = jnp.where(order >= least, value, 0.0).astype(jnp.bfloat16)
+    lat_wait(0, bands - 1, lat_sems.at[0]).wait_send()
+    for p in range(chunks):
+        some = pl.ds(0, groups - 1)
+        lev_wait(send_lev.at[p, some], recv_lev.at[p, some], lev_sems.at[p]).wait_send()
 
 
 def body(
@@ -364,13 +392,16 @@
             pltpu.VMEM((2 * levels, circles, CHUNK), f32),
             pltpu.VMEM((bands, circles, 128), bf16),
             pltpu.VMEM((bands, circles, 128), bf16),
-            pltpu.VMEM((groups, share, across), bf16),
-            pltpu.VMEM((groups, share, across), bf16),
-            pltpu.VMEM(legendre.shape, bf16),
-            pltpu.SemaphoreType.DMA((4,)),
+            pltpu.VMEM((chunks, groups, share, across // chunks), bf16),
+            pltpu.VMEM((chunks, groups, share, across // chunks), bf16),
+            pltpu.VMEM((chunks, slot_dev, across // chunks, top_wave), bf16),
+            pltpu.VMEM((groups * share, top_wave), f32),
+            pltpu.SemaphoreType.DMA((2,)),
+            pltpu.SemaphoreType.DMA((chunks,)),
+            pltpu.SemaphoreType.DMA((chunks,)),
             pltpu.SemaphoreType.DMA((4,)),
             pltpu.SemaphoreType.DMA((10,)),
-            pltpu.SemaphoreType.DMA,
+            pltpu.SemaphoreType.DMA((chunks, slot_dev)),
         ],
         compiler_params=pltpu.CompilerParams(
             vmem_limit_bytes=56 * 1024 * 1024, collective_id=0, has_side_effects=True

time: 50.4 us -> 48.7 us (0.966)
  Pallas kernels: 48.4 us -> 46.7 us
    pallas_call x1, Pallas kernels: 48.4 us -> 46.7 us  [body(): pl.pallas_call(functools.partial(whole_kernel, top_wave, bands, groups, s...]
where the time goes in v4:
time: 48.7 us; the launch traced here: 48.5 us
  Pallas kernels  46.7 us (96%)
  local copies, waits for them, and re-layouts  1.82 us (4%)
    pallas_call x1, Pallas kernels, body(): pl.pallas_call(functools.partial(whole_kernel, top_wave, bands, groups, s...  46.7 us
    reshape x1, local copies, waits for them, and re-layouts, body(): return spectra.reshape(groups * levels, 2, slot_dev, top_wave)  1.82 us

profile of v4, /device:TPU:1, one launch (start us, length us, event | category | flops | bytes accessed | tf_op | source)
XLA Modules:
  0.0 48.5 jit_solution(3455530165800353428)
XLA Ops:
  0.0 46.7 %interpolate_transform_exchange.1 = bf16[128,1280]{1,0:T(8,128)(2,1)} custom-call(bf16[2,640,128]{2,1,0:T(8,128)(2,1)} %grid_ref.1, s32[1,2,128]{2,1,0:T(2,128)} %send_ref.1, s32[2,640]{1,0:T(2,128)} %bitcast.4, s32[2,640]{1,0:T(2,128)} %bitcast.5, bf16[8,128,128]{2,1,0:T(8,128)(2,1)} %kern_ref.1, s32[768]{0:T(1024)} %len_hbm.1, s32[1536]{0:T(1024)} %wave_hbm.1, ...), custom_call_target="tpu_custom_call" | custom-call | tf_op jit(solution)/shard_map/interpolate_transform_exchange/pallas_call | solution.py:371
  46.7 1.8 %reshape.7 = bf16[32,2,2,1280]{3,2,1,0:T(2,128)(2,1)} reshape(bf16[128,1280]{1,0:T(8,128)(2,1)} %interpolate_transform_exchange.1) | data formatting | bytes 655360 | tf_op jit(solution)/shard_map/reshape | solution.py:414

commit v5 on v4

--- a/solution.py
+++ b/solution.py
@@ -56,9 +56,9 @@
             hot = jnp.where(spots == part[:, k : k + 1], 1.0, 0.0).astype(jnp.bfloat16)
             picked = jnp.dot(hot, pool_scr[...], preferred_element_type=jnp.float32)
             which = part[:, 2 + k : 3 + k]
-            for t in range(tiles):
-                chosen = jnp.where(which == float(t), picked, 0.0).astype(jnp.bfloat16)
-                total += jnp.dot(chosen, diag_scr[t], preferred_element_type=jnp.float32)
+            chosen = [jnp.where(which == float(t), picked, 0.0).astype(jnp.bfloat16) for t in range(tiles)]
+            chosen = jnp.concatenate(chosen, axis=1)
+            total += jnp.dot(chosen, diag_scr[...].reshape(tiles * width, width), preferred_element_type=jnp.float32)
         squared = total * total
         for c in range(group):
             n = len_ref[band * circles + start + c]
@@ -90,15 +90,13 @@
         table_scr[chunk, g, :, part * CHUNK : (part + 1) * CHUNK] = table
 
 
-def transform_circle(g, chunk, wave, top_wave, levels, per_circle, x_scr, len_scr, table_scr, outer_scr, coef_scr):
-    length = len_scr[pl.ds(g, 1), :]
+def transform_circle(g, chunk, levels, per_circle, x_scr, table_scr, outer_scr, coef_scr):
     outer = (outer_scr[chunk, g, 0:8, :], outer_scr[chunk, g, 8:16, :])
     jump = times((outer[0][7:8], outer[1][7:8]), (outer[0][1:2], outer[1][1:2]))
     jump = (jnp.broadcast_to(jump[0], (8, CHUNK)), jnp.broadcast_to(jump[1], (8, CHUNK)))
     x = x_scr[g]
     real = jnp.dot(x, table_scr[chunk, g, :, :CHUNK], preferred_element_type=jnp.float32)
     imag = jnp.dot(x, table_scr[chunk, g, :, CHUNK:], preferred_element_type=jnp.float32)
-    live = (wave >= 1.0) & (wave < float(top_wave)) & (2.0 * wave < length)
     for l in range(levels):
         last = per_circle // 8 - 1
         at = 48 * l + 8 * last
@@ -109,15 +107,23 @@
             total = (turned[0] + real[at : at + 8], turned[1] + imag[at : at + 8])
         total = times(total, outer)
         for c in range(2):
-            value = jnp.sum(total[c], axis=0, keepdims=True)
-            coef_scr[2 * l + c, pl.ds(g, 1), :] = jnp.where(live, value, 0.0)
-
-
-def pack_tiles(first, coef_scr, send_scr):
-    circles = coef_scr.shape[1]
+            for block in range(CHUNK // 128):
+                coef_scr[2 * l + c, block, 8 * g : 8 * g + 8, :] = total[c][:, block * 128 : (block + 1) * 128]
+
+
+def pack_tiles(first, wave, top_wave, len_scr, coef_scr, send_scr):
+    circles = len_scr.shape[0]
     quarter = lax.broadcasted_iota(jnp.int32, (circles, 128), 1) // 32
     for block in range(CHUNK // 128):
-        parts = [coef_scr[k, :, block * 128 : (block + 1) * 128] for k in range(4)]
+        cols = slice(block * 128, (block + 1) * 128)
+        waves = wave[:, cols]
+        live = (waves >= 1.0) & (waves < float(top_wave)) & (2.0 * waves < len_scr[:, cols])
+        parts = []
+        for k in range(4):
+            rows = [coef_scr[k, block, pl.ds(r, circles, stride=8), :] for r in range(8)]
+            while len(rows) > 1:
+                rows = [rows[i] + rows[i + 1] for i in range(0, len(rows), 2)]
+            parts.append(jnp.where(live, rows[0], 0.0))
         for to in range(4):
             value = parts[to]
             for k in range(4):
@@ -257,15 +263,9 @@
         chunk = lax.rem(step + home, chunks)
         wave = waves_scr[chunk]
 
-        def circle(i, inner):
-            for k in range(PAIR):
-                transform_circle(
-                    i * PAIR + k, chunk, wave, top_wave, levels, per_circle, x_scr, len_scr, table_scr, outer_scr, coef_scr
-                )
-            return inner
-
-        lax.fori_loop(0, circles // PAIR, circle, 0)
-        pack_tiles(chunk * per_chunk, coef_scr, send_lat)
+        for g in range(circles):
+            transform_circle(g, chunk, levels, per_circle, x_scr, table_scr, outer_scr, coef_scr)
+        pack_tiles(chunk * per_chunk, wave, top_wave, len_scr, coef_scr, send_lat)
         for i in range(per_chunk):
             to = chunk * per_chunk + i
 
@@ -389,7 +389,7 @@
             pltpu.VMEM((circles, CHUNK), f32),
             pltpu.VMEM((chunks, circles, FINE, 2 * CHUNK), bf16),
             pltpu.VMEM((chunks, circles, 16, CHUNK), f32),
-            pltpu.VMEM((2 * levels, circles, CHUNK), f32),
+            pltpu.VMEM((2 * levels, CHUNK // 128, 8 * circles, 128), f32),
             pltpu.VMEM((bands, circles, 128), bf16),
             pltpu.VMEM((bands, circles, 128), bf16),
             pltpu.VMEM((chunks, groups, share, across // chunks), bf16),
@@ -404,12 +404,17 @@
             pltpu.SemaphoreType.DMA((chunks, slot_dev)),
         ],
         compiler_params=pltpu.CompilerParams(
-            vmem_limit_bytes=56 * 1024 * 1024, collective_id=0, has_side_effects=True
+            vmem_limit_bytes=40 * 1024 * 1024, collective_id=0, has_side_effects=True
         ),
         name="interpolate_transform_exchange",
     )(
-        grid_field, send_blocks, donor_index.T, tile_choice.T, kernel_tiles, circle_len, slot_wave,
-        slot_wave.reshape(slots // 128, 128), legendre,
+        *(
+            pltpu.with_memory_space_constraint(array, pltpu.HBM)
+            for array in (
+                grid_field, send_blocks, donor_index.T, tile_choice.T, kernel_tiles, circle_len, slot_wave,
+                slot_wave.reshape(slots // 128, 128), legendre,
+            )
+        )
     )
     return spectra.reshape(groups * levels, 2, slot_dev, top_wave)
 

time: 48.7 us -> 46.1 us (0.947)
  Pallas kernels: 46.7 us -> 45.1 us
  local copies, waits for them, and re-layouts: 1.82 us -> 0.85 us
    pallas_call x1, Pallas kernels: 46.7 us -> 45.1 us  [body(): pl.pallas_call(functools.partial(whole_kernel, top_wave, bands, groups, s...]
    reshape x1, local copies, waits for them, and re-layouts: 1.82 us -> 0.85 us  [body(): return spectra.reshape(groups * levels, 2, slot_dev, top_wave)]
where the time goes in v5:
time: 46.1 us; the launch traced here: 46 us
  Pallas kernels  45.1 us (98%)
  local copies, waits for them, and re-layouts  0.85 us (2%)
    pallas_call x1, Pallas kernels, body(): pl.pallas_call(functools.partial(whole_kernel, top_wave, bands, groups, s...  45.1 us

profile of v5, /device:TPU:1, one launch (start us, length us, event | category | flops | bytes accessed | tf_op | source)
XLA Modules:
  0.0 46.0 jit_solution(4866601114217985805)
XLA Ops:
  0.0 45.1 %interpolate_transform_exchange.1 = bf16[128,1280]{1,0:T(8,128)(2,1)S(1)} custom-call(bf16[2,640,128]{2,1,0:T(8,128)(2,1)} %grid_ref.1, s32[1,2,128]{2,1,0:T(2,128)} %send_ref.1, s32[2,640]{1,0:T(2,128)} %bitcast.4, s32[2,640]{1,0:T(2,128)} %bitcast.5, bf16[8,128,128]{2,1,0:T(8,128)(2,1)} %kern_ref.1, s32[768]{0:T(1024)} %len_hbm.1, s32[1536]{0:T(1024)} %wave_hbm.1, ...), custom_call_target="tpu_custom_call" | custom-call | tf_op jit(solution)/shard_map/interpolate_transform_exchange/pallas_call | solution.py:371
  45.1 0.8 %reshape.7 = bf16[32,2,2,1280]{3,2,1,0:T(2,128)(2,1)} reshape(bf16[128,1280]{1,0:T(8,128)(2,1)S(1)} %interpolate_transform_exchange.1) | data formatting | bytes 655360 | tf_op jit(solution)/shard_map/reshape | solution.py:419

commit v6 on v5

--- a/solution.py
+++ b/solution.py
@@ -11,7 +11,7 @@
 FINE = 128
 CHUNK = 256
 PAIR = 8
-EARLY = 4
+EARLY = 6
 
 SIN_COEF = (3.1415927410125732, -5.167709827423096, 2.550076961517334, -0.5982874631881714, 0.07764891535043716)
 COS_COEF = (1.0, -4.934792518615723, 4.058409690856934, -1.331863284111023, 0.21965928375720978)
@@ -144,6 +144,19 @@
     circles = x_scr.shape[0]
     per_circle = blocks // circles
     band, group = lax.axis_index("lat"), lax.axis_index("lev")
+    barrier = pltpu.get_barrier_semaphore()
+
+    def greet_lat(i, carry):
+        pl.semaphore_signal(barrier, inc=1, device_id={"lat": lax.rem(band + i, bands)}, device_id_type=MESH)
+        return carry
+
+    def greet_lev(i, carry):
+        pl.semaphore_signal(barrier, inc=1, device_id={"lev": lax.rem(group + i, groups)}, device_id_type=MESH)
+        return carry
+
+    lax.fori_loop(1, bands, greet_lat, 0)
+    lax.fori_loop(1, groups, greet_lev, 0)
+
     pairs = [(len_hbm, len_ref), (wave_rows_ref, wave_scr), (send_ref, send_scr), (donor_ref, donor_scr), (tile_ref, tile_scr)]
     for l in range(levels):
         cols = slice(l * lanes, (l + 1) * lanes)
@@ -162,19 +175,6 @@
             fetches.append(pltpu.make_async_copy(legendre_ref.at[k, rows], leg_scr.at[p, k], leg_sems.at[p, k]))
     for fetch in fetches:
         fetch.start()
-    barrier = pltpu.get_barrier_semaphore()
-
-    def greet_lat(i, carry):
-        pl.semaphore_signal(barrier, inc=1, device_id={"lat": lax.rem(band + i, bands)}, device_id_type=MESH)
-        return carry
-
-    def greet_lev(i, carry):
-        pl.semaphore_signal(barrier, inc=1, device_id={"lev": lax.rem(group + i, groups)}, device_id_type=MESH)
-        return carry
-
-    lax.fori_loop(1, bands, greet_lat, 0)
-    lax.fori_loop(1, groups, greet_lev, 0)
-
     for l in range(levels):
         for m in range(levels):
             if l != m:
@@ -260,7 +260,7 @@
     home = band // per_chunk
 
     def chunk_step(step, carry):
-        chunk = lax.rem(step + home, chunks)
+        chunk = lax.rem(step + 1 + home, chunks)
         wave = waves_scr[chunk]
 
         for g in range(circles):
@@ -302,8 +302,8 @@
     pick = jnp.where(source == wanted, 1.0, 0.0).astype(jnp.bfloat16)
     span = per_chunk * circles
     for p in range(chunks):
-        part = lax.rem(home + chunks - p, chunks)
-        lat_wait(part * per_chunk, per_chunk - (p == 0), lat_sems.at[part]).wait_recv()
+        part = lax.rem(home + chunks - 1 - p, chunks)
+        lat_wait(part * per_chunk, per_chunk - (p == chunks - 1), lat_sems.at[part]).wait_recv()
         arrived = recv_lat[pl.ds(part * per_chunk, per_chunk)].reshape(span, 128)
         turned = lax.dot_general(pick, arrived, (((1,), (1,)), ((), ())), preferred_element_type=jnp.float32)
         for v in range(groups):
@@ -326,7 +326,7 @@
     width = 256
     kinds = lax.broadcasted_iota(jnp.int32, (128, span), 0) % slot_dev
     for p in range(chunks):
-        part = lax.rem(home + chunks - p, chunks)
+        part = lax.rem(home + chunks - 1 - p, chunks)
         some = pl.ds(0, groups - 1)
         lev_wait(send_lev.at[p, some], recv_lev.at[p, some], lev_sems.at[p]).wait_recv()
         left = jnp.concatenate([recv_lev[p, v].astype(jnp.float32) for v in range(groups)], axis=0)

time: 46.1 us -> 46.8 us (1.015)
  Pallas kernels: 45.1 us -> 45.8 us
    pallas_call x1, Pallas kernels: 45.1 us -> 45.8 us  [body(): pl.pallas_call(functools.partial(whole_kernel, top_wave, bands, groups, s...]
where the time goes in v6:
time: 46.8 us; the launch traced here: 46.7 us
  Pallas kernels  45.8 us (98%)
  local copies, waits for them, and re-layouts  0.85 us (2%)
    pallas_call x1, Pallas kernels, body(): pl.pallas_call(functools.partial(whole_kernel, top_wave, bands, groups, s...  45.8 us

profile of v6, /device:TPU:1, one launch (start us, length us, event | category | flops | bytes accessed | tf_op | source)
XLA Modules:
  0.0 46.7 jit_solution(2407108846541011370)
XLA Ops:
  0.0 45.8 %interpolate_transform_exchange.1 = bf16[128,1280]{1,0:T(8,128)(2,1)S(1)} custom-call(bf16[2,640,128]{2,1,0:T(8,128)(2,1)} %grid_ref.1, s32[1,2,128]{2,1,0:T(2,128)} %send_ref.1, s32[2,640]{1,0:T(2,128)} %bitcast.4, s32[2,640]{1,0:T(2,128)} %bitcast.5, bf16[8,128,128]{2,1,0:T(8,128)(2,1)} %kern_ref.1, s32[768]{0:T(1024)} %len_hbm.1, s32[1536]{0:T(1024)} %wave_hbm.1, ...), custom_call_target="tpu_custom_call" | custom-call | tf_op jit(solution)/shard_map/interpolate_transform_exchange/pallas_call | solution.py:371
  45.8 0.8 %reshape.7 = bf16[32,2,2,1280]{3,2,1,0:T(2,128)(2,1)} reshape(bf16[128,1280]{1,0:T(8,128)(2,1)S(1)} %interpolate_transform_exchange.1) | data formatting | bytes 655360 | tf_op jit(solution)/shard_map/reshape | solution.py:419
